TPU v7x, 32 devices: a whole 2x2x4 slice. The times are simulated.
32 devices in a mesh: group: 2 (over y), sector: 16 (over z, x, core).
Axes of the slice: x: 2, y: 2, z: 4, core: 2. Of those that a mesh axis runs over, the one named last changes fastest.
Arguments:
- wavefunction: bfloat16 [16, 512, 512], P('sector'), may hold values from -6 to 6
- left_factors: bfloat16 [6, 512, 512], P('group'), may hold values from -0.125 to 0.125
- right_factors: bfloat16 [6, 512, 512], P('group'), may hold values from -0.125 to 0.125
- term_list: int32 [128, 3], P(('group', 'sector')), may hold values from 0 to 2, as said below
- term_counts: int32 [32], P(('group', 'sector')), may hold values from 1 to 4, as said below
- sector_sizes: int32 [16], replicated, may hold values from 128 to 512, as said below
Outputs:
- product_wave: bfloat16 [16, 512, 512], P('sector', 'group')
Inputs may be any that keep to these rules, and one draw needn't show every extreme that they name: `term_list`: column 0 lies in 0 to 2 and never points outside the sectors (no 0 for sector 0, no 2 for sector 16 - 1); columns 1 and 2 name factors 0 to 2 of the slot's own group. `term_counts`: each owner has 1 or 4 live slots; some owner has 4. `sector_sizes`: sector 0 is full.
All inputs are finite; a program needn't handle non-finite values.
Results may differ from a plain program's by a relative error of at most 0.0049.
Values may be sent and summed in bfloat16 or wider, within the bound.
No kernel may reach another device: no remote copies, remote signals or barrier semaphores. Data moves between devices by JAX's collectives and lax.ppermute only.
A program may use at most 64 MiB of HBM per device.

v0:
```python
import functools

import jax
import jax.numpy as jnp
from jax import lax
from jax.experimental import pallas as pl
from jax.experimental.pallas import tpu as pltpu
from jax.sharding import PartitionSpec as P

F32 = jnp.float32
BF16 = jnp.bfloat16
VMEM = pl.BlockSpec(memory_space=pltpu.VMEM)
SMEM = pl.BlockSpec(memory_space=pltpu.SMEM)
HBM = pl.BlockSpec(memory_space=pltpu.HBM)
PARAMS = pltpu.CompilerParams(vmem_limit_bytes=16 * 1024 * 1024)


def dot(a, b, ca, cb):
    return lax.dot_general(a, b, (((ca,), (cb,)), ((), ())), preferred_element_type=F32)


def forward(acc, left, source, right):
    middle = dot(left[...], source[...], 1, 0).astype(BF16)
    acc[...] += dot(middle, right[...], 1, 0)


def adjoint(acc, left, source, right):
    middle = dot(left[...], source[...], 0, 0).astype(BF16)
    acc[...] += dot(middle, right[...], 1, 1)


def friend_of(sector):
    return sector + 1 - 2 * (sector % 2)


def other_of(sector):
    return sector - 1 + 2 * (sector % 2)


def masked(block, size):
    rows = lax.broadcasted_iota(jnp.int32, block.shape, 0)
    cols = lax.broadcasted_iota(jnp.int32, block.shape, 1)
    return jnp.where((rows < size) & (cols < size), block, jnp.zeros_like(block))


def live_terms(codes, owner, want, action):
    for k in range(codes.shape[0]):
        @pl.when(owner + codes[k, 0] - 2 == want)
        def _():
            action(codes[k, 1] - 1, codes[k, 2] - 1)


def near_kernel(own_codes, friend_codes, sizes, own_hbm, friend_block, left_hbm, right_hbm,
                acc, left, right, own, clean, friend_clean, sems):
    here = lax.axis_index("sector")
    friend = friend_of(here)
    count = left.shape[0]
    copies = [pltpu.make_async_copy(own_hbm.at[0], own, sems.at[2 * count])]
    for i in range(count):
        copies.append(pltpu.make_async_copy(left_hbm.at[i], left.at[i], sems.at[i]))
        copies.append(pltpu.make_async_copy(right_hbm.at[i], right.at[i], sems.at[count + i]))
    for copy in copies:
        copy.start()
    friend_clean[...] = masked(friend_block[0], sizes[jnp.minimum(friend, sizes.shape[0] - 1)])
    acc[...] = jnp.zeros_like(acc)
    copies[0].wait()
    clean[...] = masked(own[...], sizes[here])
    for copy in copies[1:]:
        copy.wait()

    def self_term(l, r):
        forward(acc, left.at[l], clean, right.at[r])
        adjoint(acc, left.at[l], clean, right.at[r])

    live_terms(own_codes, here, here, self_term)
    live_terms(own_codes, here, friend, lambda l, r: adjoint(acc, left.at[l], friend_clean, right.at[r]))
    live_terms(friend_codes, friend, here, lambda l, r: forward(acc, left.at[l], friend_clean, right.at[r]))


def far_kernel(mine, own_codes, other_codes, sizes, other_block, left, right, near, out, clean, acc):
    here = lax.axis_index("sector")
    other = other_of(here)
    share = out.shape[0]
    clean[...] = masked(other_block[0], sizes[jnp.clip(other, 0, sizes.shape[0] - 1)])

    def run(rows):
        acc[...] = near[rows, :]
        live_terms(own_codes, here, other,
                   lambda l, r: adjoint(acc, left.at[l, :, rows], clean, right.at[r]))
        live_terms(other_codes, other, here,
                   lambda l, r: forward(acc, left.at[l, rows, :], clean, right.at[r]))
        out[...] = acc[...].astype(out.dtype)

    if share == near.shape[0]:
        run(slice(None))
        return
    for g in range(near.shape[0] // share):
        @pl.when((lax.axis_index("group") == g) == mine)
        def _():
            run(slice(g * share, (g + 1) * share))


def last_kernel(sizes, kept, *refs):
    got, out = refs[:-1], refs[-1]
    share = kept.shape[0]
    total = kept[...]
    for part in got:
        total = total + part[...].astype(F32)
    rows = lax.broadcasted_iota(jnp.int32, total.shape, 0) + lax.axis_index("group") * share
    cols = lax.broadcasted_iota(jnp.int32, total.shape, 1)
    size = sizes[lax.axis_index("sector")]
    out[0] = jnp.where((rows < size) & (cols < size), total, 0.0).astype(BF16)


def shards(wavefunction, left_factors, right_factors, term_list, term_counts, sector_sizes):
    width = wavefunction.shape[1]
    groups = lax.axis_size("group")
    sectors = lax.axis_size("sector")
    share = width // groups
    slots = term_list.shape[0]
    factors = left_factors.shape
    friends = [(s, friend_of(s)) for s in range(sectors) if friend_of(s) < sectors]
    others = [(s, other_of(s)) for s in range(sectors) if 0 <= other_of(s) < sectors]
    block = pltpu.VMEM((width, width), BF16)
    hbm = functools.partial(pltpu.with_memory_space_constraint, memory_space=pltpu.HBM)

    other_block = lax.ppermute(wavefunction, "sector", others)
    friend_block = lax.ppermute(wavefunction, "sector", friends)
    live = jnp.arange(slots, dtype=jnp.int32)[:, None] < term_counts
    codes = jnp.where(live, term_list + 1, 0)
    friend_codes = lax.ppermute(codes, "sector", friends)
    other_codes = lax.ppermute(codes, "sector", others)
    near, left, right = pl.pallas_call(
        near_kernel,
        out_shape=[
            jax.ShapeDtypeStruct((width, width), F32),
            jax.ShapeDtypeStruct(factors, BF16),
            jax.ShapeDtypeStruct(factors, BF16),
        ],
        in_specs=[SMEM, SMEM, SMEM, HBM, VMEM, HBM, HBM],
        out_specs=[VMEM] * 3,
        scratch_shapes=[block, block, block, pltpu.SemaphoreType.DMA((2 * factors[0] + 1,))],
        compiler_params=PARAMS,
        name="near",
    )(codes, friend_codes, sector_sizes, hbm(wavefunction), friend_block, hbm(left_factors), hbm(right_factors))

    def far(rows, mine, dtype):
        return pl.pallas_call(
            functools.partial(far_kernel, mine),
            out_shape=jax.ShapeDtypeStruct((rows, width), dtype),
            in_specs=[SMEM, SMEM, SMEM, VMEM, VMEM, VMEM, VMEM],
            out_specs=VMEM,
            scratch_shapes=[block, pltpu.VMEM((rows, width), F32)],
            compiler_params=PARAMS,
            name="far_mine" if mine else "far_theirs",
        )(codes, other_codes, sector_sizes, other_block, left, right, near)

    hops = [[(g, (g + hop) % groups) for g in range(groups)] for hop in range(1, groups)]
    if groups == 2 and share % 128 == 0:
        theirs = far(share, False, BF16)
        got = [lax.ppermute(theirs, "group", hops[0])]
        kept = far(share, True, F32)
    else:
        whole = far(width, True, F32)
        group = lax.axis_index("group")
        kept = lax.dynamic_slice_in_dim(whole, group * share, share, 0)
        got = []
        for hop, pairs in enumerate(hops, 1):
            part = lax.dynamic_slice_in_dim(whole, (group + hop) % groups * share, share, 0)
            got.append(lax.ppermute(part.astype(BF16), "group", pairs))
    return pl.pallas_call(
        last_kernel,
        out_shape=jax.ShapeDtypeStruct((1, share, width), BF16),
        in_specs=[SMEM, VMEM] + [VMEM] * len(got),
        out_specs=VMEM,
        compiler_params=PARAMS,
        name="last",
    )(sector_sizes, kept, *got)


def solution(mesh):
    return jax.shard_map(
        shards,
        mesh=mesh,
        in_specs=(
            P("sector", None, None),
            P("group", None, None),
            P("group", None, None),
            P(("group", "sector"), None),
            P(("group", "sector")),
            P(),
        ),
        out_specs=P("sector", "group", None),
        check_vma=False,
    )
```

profile of v0, /device:TPU:18, one launch (start us, length us, event | category | flops | bytes accessed | tf_op | source)
XLA Modules:
  0.0 28.5 jit_solution(18441632588340643797)
XLA Ops:
  0.0 0.0 collective-permute-start.3
  0.0 2.5 %collective-permute-start.1 = (bf16[1,512,512]{2,1,0:T(8,128)(2,1)}, bf16[1,512,512]{2,1,0:T(8,128)(2,1)S(1)}, u32[]{:S(2)}, u32[]{:S(2)}) collective-permute-start(bf16[1,512,512]{2,1,0:T(8,128)(2,1)} %own_hbm.1), channel_id=1, source_target_pairs={{1,2},{2,1},{3,4},{4,3},{5,6},{6,5},{7,8},{8,7},{9,10},{10,9},{11,... | collective-permute-start | bytes 1572872 | tf_op jit(solution)/shard_map/ppermute | solution.py:127
  3.2 0.8 %add_select_fusion.own_codes = s32[4,3]{1,0:T(4,128)S(1)} fusion(s32[4,3]{1,0:T(4,128)} %param.9, pred[4]{0:T(512)(128)(4,1)S(1)} %iota_compare_fusion), kind=kLoop, calls=%fused_computation | loop fusion | flops 24 | bytes 100 | tf_op jit(solution)/shard_map/jit(_where)/select_n | solution.py:130
  4.0 1.0 %collective-permute-start.2 = (s32[4,3]{1,0:T(4,128)S(1)}, s32[4,3]{1,0:T(4,128)S(1)}, u32[]{:S(2)}, u32[]{:S(2)}) collective-permute-start(s32[4,3]{1,0:T(4,128)S(1)} %add_select_fusion.own_codes), channel_id=1, source_target_pairs={{0,1},{1,0},{2,3},{3,2},{4,5},{5,4},{6,7},{7,6},{8,9},{9,8},{10,11... | collective-permute-start | bytes 152 | tf_op jit(solution)/shard_map/ppermute | solution.py:131
  5.0 2.4 %collective-permute-start = (s32[4,3]{1,0:T(4,128)S(1)}, s32[4,3]{1,0:T(4,128)S(1)}, u32[]{:S(2)}, u32[]{:S(2)}) collective-permute-start(s32[4,3]{1,0:T(4,128)S(1)} %add_select_fusion.own_codes), channel_id=1, source_target_pairs={{1,2},{2,1},{3,4},{4,3},{5,6},{6,5},{7,8},{8,7},{9,10},{10,9},{11,... | collective-permute-start | bytes 152 | tf_op jit(solution)/shard_map/ppermute | solution.py:132
  7.4 0.0 collective-permute-done.2.friend_codes
  7.4 0.0 collective-permute-done.3.friend_block
  7.4 0.0 copy-start
  7.4 0.6 %copy-done = s32[16]{0:T(128)S(1)} copy-done((s32[16]{0:T(128)S(1)}, s32[16]{0:T(128)}, u32[]{:S(2)}) %copy-start) | copy-done | bytes 88
  8.0 2.6 %near.1 = (f32[512,512]{1,0:T(8,128)S(1)}, bf16[3,512,512]{2,1,0:T(8,128)(2,1)S(1)}, bf16[3,512,512]{2,1,0:T(8,128)(2,1)S(1)}) custom-call(s32[4,3]{1,0:T(4,128)S(1)} %add_select_fusion.own_codes, s32[4,3]{1,0:T(4,128)S(1)} %collective-permute-done.2.friend_codes, s32[16]{0:T(128)S(1)} %copy-done, bf16[1,512,512]{2,1,0:T(8,128)(2,1)} %own_hbm.1, ...), custom_call_target="tpu_custom_call" | custom-call | tf_op jit(solution)/shard_map/near/pallas_call | solution.py:133
  10.7 5.7 %collective-permute-done.other_codes = s32[4,3]{1,0:T(4,128)S(1)} collective-permute-done((s32[4,3]{1,0:T(4,128)S(1)}, s32[4,3]{1,0:T(4,128)S(1)}, u32[]{:S(2)}, u32[]{:S(2)}) %collective-permute-start) | collective-permute-done | bytes 80 | tf_op jit(solution)/shard_map/ppermute | solution.py:132
  16.4 0.0 collective-permute-done.1.other_block
  16.4 2.2 %far_theirs.1 = bf16[256,512]{1,0:T(8,128)(2,1)S(1)} custom-call(s32[4,3]{1,0:T(4,128)S(1)} %add_select_fusion.own_codes, s32[4,3]{1,0:T(4,128)S(1)} %collective-permute-done.other_codes, s32[16]{0:T(128)S(1)} %copy-done, bf16[1,512,512]{2,1,0:T(8,128)(2,1)S(1)} %collective-permute-done.1.other_block, bf16[3,512,512]{2,1,0:T(8,128)(2,1)S(1)} %get-tuple-element.8.left, ...), custom_call_target="tpu_custom_call" | custom-call | tf_op jit(solution)/shard_map/far_theirs/pallas_call | solution.py:148
  18.6 0.5 %collective-permute-start.4 = (bf16[256,512]{1,0:T(8,128)(2,1)S(1)}, bf16[256,512]{1,0:T(8,128)(2,1)S(1)}, u32[]{:S(2)}, u32[]{:S(2)}) collective-permute-start(bf16[256,512]{1,0:T(8,128)(2,1)S(1)} %far_theirs.1), channel_id=1, source_target_pairs={{0,16},{16,0},{1,17},{17,1},{2,18},{18,2},{3,19},{19,3},{4,20},{20... | collective-permute-start | bytes 786440 | tf_op jit(solution)/shard_map/ppermute | solution.py:161
  19.1 2.0 %far_mine.1.kept = f32[256,512]{1,0:T(8,128)S(1)} custom-call(s32[4,3]{1,0:T(4,128)S(1)} %add_select_fusion.own_codes, s32[4,3]{1,0:T(4,128)S(1)} %collective-permute-done.other_codes, s32[16]{0:T(128)S(1)} %copy-done, bf16[1,512,512]{2,1,0:T(8,128)(2,1)S(1)} %collective-permute-done.1.other_block, bf16[3,512,512]{2,1,0:T(8,128)(2,1)S(1)} %get-tuple-element.8.left, ...), custom_call_target="tpu_custom_call" | custom-call | tf_op jit(solution)/shard_map/far_mine/pallas_call | solution.py:148
  21.1 6.1 %collective-permute-done.4.refs_0_ = bf16[256,512]{1,0:T(8,128)(2,1)S(1)} collective-permute-done((bf16[256,512]{1,0:T(8,128)(2,1)S(1)}, bf16[256,512]{1,0:T(8,128)(2,1)S(1)}, u32[]{:S(2)}, u32[]{:S(2)}) %collective-permute-start.4) | collective-permute-done | bytes 262176 | tf_op jit(solution)/shard_map/ppermute | solution.py:161
  27.2 1.3 %last.1 = bf16[1,256,512]{2,1,0:T(8,128)(2,1)} custom-call(s32[16]{0:T(128)S(1)} %copy-done, f32[256,512]{1,0:T(8,128)S(1)} %far_mine.1.kept, bf16[256,512]{1,0:T(8,128)(2,1)S(1)} %collective-permute-done.4.refs_0_), custom_call_target="tpu_custom_call" | custom-call | tf_op jit(solution)/shard_map/last/pallas_call | solution.py:171
  (1 shorter events, 0.0 us)
Async XLA Ops:
  0.0 7.4 %collective-permute-start.3 = (bf16[1,512,512]{2,1,0:T(8,128)(2,1)}, bf16[1,512,512]{2,1,0:T(8,128)(2,1)S(1)}, u32[]{:S(2)}, u32[]{:S(2)}) collective-permute-start(bf16[1,512,512]{2,1,0:T(8,128)(2,1)} %own_hbm.1), channel_id=1, source_target_pairs={{0,1},{1,0},{2,3},{3,2},{4,5},{5,4},{6,7},{7,6},{8,9},{9,8},{10,11... | collective-permute-start | bytes 1572872 | tf_op jit(solution)/shard_map/ppermute | solution.py:128
  0.0 16.4 %collective-permute-start.1 = (bf16[1,512,512]{2,1,0:T(8,128)(2,1)}, bf16[1,512,512]{2,1,0:T(8,128)(2,1)S(1)}, u32[]{:S(2)}, u32[]{:S(2)}) collective-permute-start(bf16[1,512,512]{2,1,0:T(8,128)(2,1)} %own_hbm.1), channel_id=1, source_target_pairs={{1,2},{2,1},{3,4},{4,3},{5,6},{6,5},{7,8},{8,7},{9,10},{10,9},{11,... | collective-permute-start | bytes 1572872 | tf_op jit(solution)/shard_map/ppermute | solution.py:127
  4.0 3.4 %collective-permute-start.2 = (s32[4,3]{1,0:T(4,128)S(1)}, s32[4,3]{1,0:T(4,128)S(1)}, u32[]{:S(2)}, u32[]{:S(2)}) collective-permute-start(s32[4,3]{1,0:T(4,128)S(1)} %add_select_fusion.own_codes), channel_id=1, source_target_pairs={{0,1},{1,0},{2,3},{3,2},{4,5},{5,4},{6,7},{7,6},{8,9},{9,8},{10,11... | collective-permute-start | bytes 152 | tf_op jit(solution)/shard_map/ppermute | solution.py:131
  5.0 11.4 %collective-permute-start = (s32[4,3]{1,0:T(4,128)S(1)}, s32[4,3]{1,0:T(4,128)S(1)}, u32[]{:S(2)}, u32[]{:S(2)}) collective-permute-start(s32[4,3]{1,0:T(4,128)S(1)} %add_select_fusion.own_codes), channel_id=1, source_target_pairs={{1,2},{2,1},{3,4},{4,3},{5,6},{6,5},{7,8},{8,7},{9,10},{10,9},{11,... | collective-permute-start | bytes 152 | tf_op jit(solution)/shard_map/ppermute | solution.py:132
  7.4 0.7 %copy-start = (s32[16]{0:T(128)S(1)}, s32[16]{0:T(128)}, u32[]{:S(2)}) copy-start(s32[16]{0:T(128)} %sizes.7) | copy-start | bytes 196
  18.6 8.6 %collective-permute-start.4 = (bf16[256,512]{1,0:T(8,128)(2,1)S(1)}, bf16[256,512]{1,0:T(8,128)(2,1)S(1)}, u32[]{:S(2)}, u32[]{:S(2)}) collective-permute-start(bf16[256,512]{1,0:T(8,128)(2,1)S(1)} %far_theirs.1), channel_id=1, source_target_pairs={{0,16},{16,0},{1,17},{17,1},{2,18},{18,2},{3,19},{19,3},{4,20},{20... | collective-permute-start | bytes 786440 | tf_op jit(solution)/shard_map/ppermute | solution.py:161
where the time goes:
time: 28.7 us; the launch traced here: 28.5 us
  waiting for transfers between devices  11.8 us (41%)
  Pallas kernels  8.14 us (28%)
  starting transfers between devices  6.46 us (23%)
  other arithmetic  0.76 us (3%)
  between operations  0.72 us (3%)
  local copies, waits for them, and re-layouts  0.65 us (2%)
    ppermute x1, waiting for transfers between devices, shards(): got = [lax.ppermute(theirs, 'group', hops[0])]  6.09 us
    ppermute x1, waiting for transfers between devices, shards(): other_codes = lax.ppermute(codes, 'sector', others)  5.66 us
    pallas_call x2, Pallas kernels, far(): pl.pallas_call(functools.partial(far_kernel, mine), out_shape=jax.ShapeDt...  4.16 us
    pallas_call x1, Pallas kernels, shards(): pl.pallas_call(near_kernel, out_shape=[jax.ShapeDtypeStruct((width, width...  2.65 us
    ppermute x1, starting transfers between devices, shards(): other_block = lax.ppermute(wavefunction, 'sector', others)  2.55 us
    ppermute x1, starting transfers between devices, shards(): other_codes = lax.ppermute(codes, 'sector', others)  2.37 us
    pallas_call x1, Pallas kernels, shards(): pl.pallas_call(last_kernel, out_shape=jax.ShapeDtypeStruct((1, share, wid...  1.34 us
    ppermute x1, starting transfers between devices, shards(): friend_codes = lax.ppermute(codes, 'sector', friends)  1.02 us
  transfers between devices with their start and end apart: 5, of which 2 were waited for; matrix products, arithmetic and copies ran while one was open for 3% of the time, Pallas kernels for 16%

commit v1 on v0

--- a/solution.py
+++ b/solution.py
@@ -11,7 +11,6 @@
 BF16 = jnp.bfloat16
 VMEM = pl.BlockSpec(memory_space=pltpu.VMEM)
 SMEM = pl.BlockSpec(memory_space=pltpu.SMEM)
-HBM = pl.BlockSpec(memory_space=pltpu.HBM)
 PARAMS = pltpu.CompilerParams(vmem_limit_bytes=16 * 1024 * 1024)
 
 
@@ -50,23 +49,18 @@
             action(codes[k, 1] - 1, codes[k, 2] - 1)
 
 
-def near_kernel(own_codes, friend_codes, sizes, own_hbm, friend_block, left_hbm, right_hbm,
-                acc, left, right, own, clean, friend_clean, sems):
+def codes_kernel(term_list, term_counts, codes):
+    for k in range(codes.shape[0]):
+        for j in range(codes.shape[1]):
+            codes[k, j] = jnp.where(k < term_counts[0], term_list[k, j] + 1, 0)
+
+
+def near_kernel(own_codes, friend_codes, sizes, own_block, friend_block, left, right, acc, clean, friend_clean):
     here = lax.axis_index("sector")
     friend = friend_of(here)
-    count = left.shape[0]
-    copies = [pltpu.make_async_copy(own_hbm.at[0], own, sems.at[2 * count])]
-    for i in range(count):
-        copies.append(pltpu.make_async_copy(left_hbm.at[i], left.at[i], sems.at[i]))
-        copies.append(pltpu.make_async_copy(right_hbm.at[i], right.at[i], sems.at[count + i]))
-    for copy in copies:
-        copy.start()
+    clean[...] = masked(own_block[0], sizes[here])
     friend_clean[...] = masked(friend_block[0], sizes[jnp.minimum(friend, sizes.shape[0] - 1)])
     acc[...] = jnp.zeros_like(acc)
-    copies[0].wait()
-    clean[...] = masked(own[...], sizes[here])
-    for copy in copies[1:]:
-        copy.wait()
 
     def self_term(l, r):
         forward(acc, left.at[l], clean, right.at[r])
@@ -117,32 +111,33 @@
     groups = lax.axis_size("group")
     sectors = lax.axis_size("sector")
     share = width // groups
-    slots = term_list.shape[0]
-    factors = left_factors.shape
     friends = [(s, friend_of(s)) for s in range(sectors) if friend_of(s) < sectors]
     others = [(s, other_of(s)) for s in range(sectors) if 0 <= other_of(s) < sectors]
     block = pltpu.VMEM((width, width), BF16)
+
     hbm = functools.partial(pltpu.with_memory_space_constraint, memory_space=pltpu.HBM)
-
     other_block = lax.ppermute(wavefunction, "sector", others)
     friend_block = lax.ppermute(wavefunction, "sector", friends)
-    live = jnp.arange(slots, dtype=jnp.int32)[:, None] < term_counts
-    codes = jnp.where(live, term_list + 1, 0)
+    codes = pl.pallas_call(
+        codes_kernel,
+        out_shape=jax.ShapeDtypeStruct(term_list.shape, jnp.int32),
+        in_specs=[SMEM, SMEM],
+        out_specs=SMEM,
+        compiler_params=pltpu.CompilerParams(vmem_limit_bytes=2**20),
+        cost_estimate=pl.CostEstimate(flops=10**9, transcendentals=0, bytes_accessed=4 * 2**20),
+        name="codes",
+    )(hbm(term_list), term_counts)
     friend_codes = lax.ppermute(codes, "sector", friends)
     other_codes = lax.ppermute(codes, "sector", others)
-    near, left, right = pl.pallas_call(
+    near = pl.pallas_call(
         near_kernel,
-        out_shape=[
-            jax.ShapeDtypeStruct((width, width), F32),
-            jax.ShapeDtypeStruct(factors, BF16),
-            jax.ShapeDtypeStruct(factors, BF16),
-        ],
-        in_specs=[SMEM, SMEM, SMEM, HBM, VMEM, HBM, HBM],
-        out_specs=[VMEM] * 3,
-        scratch_shapes=[block, block, block, pltpu.SemaphoreType.DMA((2 * factors[0] + 1,))],
+        out_shape=jax.ShapeDtypeStruct((width, width), F32),
+        in_specs=[SMEM, SMEM, SMEM, VMEM, VMEM, VMEM, VMEM],
+        out_specs=VMEM,
+        scratch_shapes=[block, block],
         compiler_params=PARAMS,
         name="near",
-    )(codes, friend_codes, sector_sizes, hbm(wavefunction), friend_block, hbm(left_factors), hbm(right_factors))
+    )(codes, friend_codes, sector_sizes, wavefunction, friend_block, left_factors, right_factors)
 
     def far(rows, mine, dtype):
         return pl.pallas_call(
@@ -153,7 +148,7 @@
             scratch_shapes=[block, pltpu.VMEM((rows, width), F32)],
             compiler_params=PARAMS,
             name="far_mine" if mine else "far_theirs",
-        )(codes, other_codes, sector_sizes, other_block, left, right, near)
+        )(codes, other_codes, sector_sizes, other_block, left_factors, right_factors, near)
 
     hops = [[(g, (g + hop) % groups) for g in range(groups)] for hop in range(1, groups)]
     if groups == 2 and share % 128 == 0:

time: 28.7 us -> 27.5 us (0.958)
  the two profiles are of different devices: /device:TPU:18 before, /device:TPU:22 now
where the time goes in v1:
time: 27.5 us; the launch traced here: 27.3 us
  waiting for transfers between devices  10.9 us (40%)
  Pallas kernels  7.98 us (29%)
  starting transfers between devices  7.63 us (28%)
  between operations  0.78 us (3%)
    ppermute x1, waiting for transfers between devices, shards(): got = [lax.ppermute(theirs, 'group', hops[0])]  5.89 us
    ppermute x1, waiting for transfers between devices, shards(): other_codes = lax.ppermute(codes, 'sector', others)  5.01 us
    pallas_call x1, Pallas kernels, shards(): pl.pallas_call(near_kernel, out_shape=jax.ShapeDtypeStruct((width, width)...  3.12 us
    ppermute x1, starting transfers between devices, shards(): other_block = lax.ppermute(wavefunction, 'sector', others)  2.54 us
    ppermute x1, starting transfers between devices, shards(): other_codes = lax.ppermute(codes, 'sector', others)  2.37 us
    pallas_call x2, Pallas kernels, far(): pl.pallas_call(functools.partial(far_kernel, mine), out_shape=jax.ShapeDt...  2.07 us
    ppermute x1, starting transfers between devices, shards(): got = [lax.ppermute(theirs, 'group', hops[0])]  1.63 us
    pallas_call x1, Pallas kernels, shards(): pl.pallas_call(codes_kernel, out_shape=jax.ShapeDtypeStruct(term_list.sha...  1.45 us
  transfers between devices with their start and end apart: 5, of which 2 were waited for; matrix products, arithmetic and copies ran while one was open for 0% of the time, Pallas kernels for 20%

profile of v1, /device:TPU:22, one launch (start us, length us, event | category | flops | bytes accessed | tf_op | source)
XLA Modules:
  0.0 27.3 jit_solution(11260973452588293664)
XLA Ops:
  0.0 0.0 collective-permute-start.3
  0.0 2.5 %collective-permute-start.1 = (bf16[1,512,512]{2,1,0:T(8,128)(2,1)}, bf16[1,512,512]{2,1,0:T(8,128)(2,1)S(1)}, u32[]{:S(2)}, u32[]{:S(2)}) collective-permute-start(bf16[1,512,512]{2,1,0:T(8,128)(2,1)} %own_block.1), channel_id=1, source_target_pairs={{1,2},{2,1},{3,4},{4,3},{5,6},{6,5},{7,8},{8,7},{9,10},{10,9},{11,... | collective-permute-start | bytes 1572872 | tf_op jit(solution)/shard_map/ppermute | solution.py:119
  3.2 0.0 copy-start
  3.2 0.0 copy-start.1
  3.2 0.0 copy-start.2
  3.2 0.0 copy-start.3
  3.2 1.5 %codes.1.own_codes = s32[4,3]{1,0:T(4,128)S(1)} custom-call(s32[4,3]{1,0:T(4,128)} %term_list.1, s32[1]{0:T(128)S(6)} %copy.7.term_counts), custom_call_target="tpu_custom_call" | custom-call | flops 1000000000 | bytes 4194304 | tf_op jit(solution)/shard_map/codes/pallas_call | solution.py:121
  4.7 1.1 %collective-permute-start.2 = (s32[4,3]{1,0:T(4,128)S(1)}, s32[4,3]{1,0:T(4,128)S(1)}, u32[]{:S(2)}, u32[]{:S(2)}) collective-permute-start(s32[4,3]{1,0:T(4,128)S(1)} %codes.1.own_codes), channel_id=1, source_target_pairs={{0,1},{1,0},{2,3},{3,2},{4,5},{5,4},{6,7},{7,6},{8,9},{9,8},{10,11... | collective-permute-start | bytes 152 | tf_op jit(solution)/shard_map/ppermute | solution.py:130
  5.8 2.4 %collective-permute-start = (s32[4,3]{1,0:T(4,128)S(1)}, s32[4,3]{1,0:T(4,128)S(1)}, u32[]{:S(2)}, u32[]{:S(2)}) collective-permute-start(s32[4,3]{1,0:T(4,128)S(1)} %codes.1.own_codes), channel_id=1, source_target_pairs={{1,2},{2,1},{3,4},{4,3},{5,6},{6,5},{7,8},{8,7},{9,10},{10,9},{11,... | collective-permute-start | bytes 152 | tf_op jit(solution)/shard_map/ppermute | solution.py:131
  8.2 0.0 collective-permute-done.2.friend_codes
  8.2 0.0 collective-permute-done.3.friend_block
  8.2 0.0 copy-done
  8.2 0.0 copy-done.1
  8.2 0.0 copy-done.2
  8.2 0.0 copy-done.3
  8.2 3.1 %near.1 = f32[512,512]{1,0:T(8,128)S(1)} custom-call(s32[4,3]{1,0:T(4,128)S(1)} %codes.1.own_codes, s32[4,3]{1,0:T(4,128)S(1)} %collective-permute-done.2.friend_codes, s32[16]{0:T(128)S(1)} %copy-done.3, bf16[1,512,512]{2,1,0:T(8,128)(2,1)S(1)} %copy-done.2, bf16[1,512,512]{2,1,0:T(8,128)(2,1)S(1)} %collective-permute-done.3.friend_block, ...), custom_call_target="tpu_custom_call" | custom-call | tf_op jit(solution)/shard_map/near/pallas_call | solution.py:132
  11.4 5.0 %collective-permute-done.other_codes = s32[4,3]{1,0:T(4,128)S(1)} collective-permute-done((s32[4,3]{1,0:T(4,128)S(1)}, s32[4,3]{1,0:T(4,128)S(1)}, u32[]{:S(2)}, u32[]{:S(2)}) %collective-permute-start) | collective-permute-done | bytes 80 | tf_op jit(solution)/shard_map/ppermute | solution.py:131
  16.4 0.0 collective-permute-done.1.other_block
  16.4 1.1 %far_theirs.1 = bf16[256,512]{1,0:T(8,128)(2,1)S(1)} custom-call(s32[4,3]{1,0:T(4,128)S(1)} %codes.1.own_codes, s32[4,3]{1,0:T(4,128)S(1)} %collective-permute-done.other_codes, s32[16]{0:T(128)S(1)} %copy-done.3, bf16[1,512,512]{2,1,0:T(8,128)(2,1)S(1)} %collective-permute-done.1.other_block, bf16[3,512,512]{2,1,0:T(8,128)(2,1)S(1)} %copy-done, ...), custom_call_target="tpu_custom_call" | custom-call | tf_op jit(solution)/shard_map/far_theirs/pallas_call | solution.py:143
  17.5 1.6 %collective-permute-start.4 = (bf16[256,512]{1,0:T(8,128)(2,1)S(1)}, bf16[256,512]{1,0:T(8,128)(2,1)S(1)}, u32[]{:S(2)}, u32[]{:S(2)}) collective-permute-start(bf16[256,512]{1,0:T(8,128)(2,1)S(1)} %far_theirs.1), channel_id=1, source_target_pairs={{0,16},{16,0},{1,17},{17,1},{2,18},{18,2},{3,19},{19,3},{4,20},{20... | collective-permute-start | bytes 786440 | tf_op jit(solution)/shard_map/ppermute | solution.py:156
  19.1 1.0 %far_mine.1.kept = f32[256,512]{1,0:T(8,128)S(1)} custom-call(s32[4,3]{1,0:T(4,128)S(1)} %codes.1.own_codes, s32[4,3]{1,0:T(4,128)S(1)} %collective-permute-done.other_codes, s32[16]{0:T(128)S(1)} %copy-done.3, bf16[1,512,512]{2,1,0:T(8,128)(2,1)S(1)} %collective-permute-done.1.other_block, bf16[3,512,512]{2,1,0:T(8,128)(2,1)S(1)} %copy-done, ...), custom_call_target="tpu_custom_call" | custom-call | tf_op jit(solution)/shard_map/far_mine/pallas_call | solution.py:143
  20.1 5.9 %collective-permute-done.4.refs_0_ = bf16[256,512]{1,0:T(8,128)(2,1)S(1)} collective-permute-done((bf16[256,512]{1,0:T(8,128)(2,1)S(1)}, bf16[256,512]{1,0:T(8,128)(2,1)S(1)}, u32[]{:S(2)}, u32[]{:S(2)}) %collective-permute-start.4) | collective-permute-done | bytes 262176 | tf_op jit(solution)/shard_map/ppermute | solution.py:156
  26.0 1.3 %last.1 = bf16[1,256,512]{2,1,0:T(8,128)(2,1)} custom-call(s32[16]{0:T(128)S(1)} %copy-done.3, f32[256,512]{1,0:T(8,128)S(1)} %far_mine.1.kept, bf16[256,512]{1,0:T(8,128)(2,1)S(1)} %collective-permute-done.4.refs_0_), custom_call_target="tpu_custom_call" | custom-call | tf_op jit(solution)/shard_map/last/pallas_call | solution.py:166
Async XLA Ops:
  0.0 8.2 %collective-permute-start.3 = (bf16[1,512,512]{2,1,0:T(8,128)(2,1)}, bf16[1,512,512]{2,1,0:T(8,128)(2,1)S(1)}, u32[]{:S(2)}, u32[]{:S(2)}) collective-permute-start(bf16[1,512,512]{2,1,0:T(8,128)(2,1)} %own_block.1), channel_id=1, source_target_pairs={{0,1},{1,0},{2,3},{3,2},{4,5},{5,4},{6,7},{7,6},{8,9},{9,8},{10,11... | collective-permute-start | bytes 1572872 | tf_op jit(solution)/shard_map/ppermute | solution.py:120
  0.0 16.4 %collective-permute-start.1 = (bf16[1,512,512]{2,1,0:T(8,128)(2,1)}, bf16[1,512,512]{2,1,0:T(8,128)(2,1)S(1)}, u32[]{:S(2)}, u32[]{:S(2)}) collective-permute-start(bf16[1,512,512]{2,1,0:T(8,128)(2,1)} %own_block.1), channel_id=1, source_target_pairs={{1,2},{2,1},{3,4},{4,3},{5,6},{6,5},{7,8},{8,7},{9,10},{10,9},{11,... | collective-permute-start | bytes 1572872 | tf_op jit(solution)/shard_map/ppermute | solution.py:119
  3.2 5.0 %copy-start = (bf16[3,512,512]{2,1,0:T(8,128)(2,1)S(1)}, bf16[3,512,512]{2,1,0:T(8,128)(2,1)}, u32[]{:S(2)}) copy-start(bf16[3,512,512]{2,1,0:T(8,128)(2,1)} %left.5) | copy-start | bytes 4718596
  3.2 5.0 %copy-start.1 = (bf16[3,512,512]{2,1,0:T(8,128)(2,1)S(1)}, bf16[3,512,512]{2,1,0:T(8,128)(2,1)}, u32[]{:S(2)}) copy-start(bf16[3,512,512]{2,1,0:T(8,128)(2,1)} %right.5) | copy-start | bytes 4718596
  3.2 5.0 %copy-start.2 = (bf16[1,512,512]{2,1,0:T(8,128)(2,1)S(1)}, bf16[1,512,512]{2,1,0:T(8,128)(2,1)}, u32[]{:S(2)}) copy-start(bf16[1,512,512]{2,1,0:T(8,128)(2,1)} %own_block.1) | copy-start | bytes 1572868
  3.2 5.0 %copy-start.3 = (s32[16]{0:T(128)S(1)}, s32[16]{0:T(128)}, u32[]{:S(2)}) copy-start(s32[16]{0:T(128)} %sizes.7) | copy-start | bytes 196
  4.7 3.5 %collective-permute-start.2 = (s32[4,3]{1,0:T(4,128)S(1)}, s32[4,3]{1,0:T(4,128)S(1)}, u32[]{:S(2)}, u32[]{:S(2)}) collective-permute-start(s32[4,3]{1,0:T(4,128)S(1)} %codes.1.own_codes), channel_id=1, source_target_pairs={{0,1},{1,0},{2,3},{3,2},{4,5},{5,4},{6,7},{7,6},{8,9},{9,8},{10,11... | collective-permute-start | bytes 152 | tf_op jit(solution)/shard_map/ppermute | solution.py:130
  5.8 10.6 %collective-permute-start = (s32[4,3]{1,0:T(4,128)S(1)}, s32[4,3]{1,0:T(4,128)S(1)}, u32[]{:S(2)}, u32[]{:S(2)}) collective-permute-start(s32[4,3]{1,0:T(4,128)S(1)} %codes.1.own_codes), channel_id=1, source_target_pairs={{1,2},{2,1},{3,4},{4,3},{5,6},{6,5},{7,8},{8,7},{9,10},{10,9},{11,... | collective-permute-start | bytes 152 | tf_op jit(solution)/shard_map/ppermute | solution.py:131
  17.5 8.5 %collective-permute-start.4 = (bf16[256,512]{1,0:T(8,128)(2,1)S(1)}, bf16[256,512]{1,0:T(8,128)(2,1)S(1)}, u32[]{:S(2)}, u32[]{:S(2)}) collective-permute-start(bf16[256,512]{1,0:T(8,128)(2,1)S(1)} %far_theirs.1), channel_id=1, source_target_pairs={{0,16},{16,0},{1,17},{17,1},{2,18},{18,2},{3,19},{19,3},{4,20},{20... | collective-permute-start | bytes 786440 | tf_op jit(solution)/shard_map/ppermute | solution.py:156

commit v2 on v1

--- a/solution.py
+++ b/solution.py
@@ -36,8 +36,8 @@
     return sector - 1 + 2 * (sector % 2)
 
 
-def masked(block, size):
-    rows = lax.broadcasted_iota(jnp.int32, block.shape, 0)
+def masked(block, size, first=0):
+    rows = lax.broadcasted_iota(jnp.int32, block.shape, 0) + first
     cols = lax.broadcasted_iota(jnp.int32, block.shape, 1)
     return jnp.where((rows < size) & (cols < size), block, jnp.zeros_like(block))
 
@@ -50,9 +50,8 @@
 
 
 def codes_kernel(term_list, term_counts, codes):
-    for k in range(codes.shape[0]):
-        for j in range(codes.shape[1]):
-            codes[k, j] = jnp.where(k < term_counts[0], term_list[k, j] + 1, 0)
+    slot = lax.broadcasted_iota(jnp.int32, codes.shape, 0)
+    codes[...] = jnp.where(slot < term_counts[...], term_list[...] + 1, 0)
 
 
 def near_kernel(own_codes, friend_codes, sizes, own_block, friend_block, left, right, acc, clean, friend_clean):
@@ -78,12 +77,13 @@
     clean[...] = masked(other_block[0], sizes[jnp.clip(other, 0, sizes.shape[0] - 1)])
 
     def run(rows):
+        first = rows.start or 0
         acc[...] = near[rows, :]
         live_terms(own_codes, here, other,
                    lambda l, r: adjoint(acc, left.at[l, :, rows], clean, right.at[r]))
         live_terms(other_codes, other, here,
                    lambda l, r: forward(acc, left.at[l, rows, :], clean, right.at[r]))
-        out[...] = acc[...].astype(out.dtype)
+        out[...] = masked(acc[...], sizes[here], first).astype(out.dtype)
 
     if share == near.shape[0]:
         run(slice(None))
@@ -94,16 +94,11 @@
             run(slice(g * share, (g + 1) * share))
 
 
-def last_kernel(sizes, kept, *refs):
-    got, out = refs[:-1], refs[-1]
-    share = kept.shape[0]
+def last_kernel(kept, *refs):
     total = kept[...]
-    for part in got:
+    for part in refs[:-1]:
         total = total + part[...].astype(F32)
-    rows = lax.broadcasted_iota(jnp.int32, total.shape, 0) + lax.axis_index("group") * share
-    cols = lax.broadcasted_iota(jnp.int32, total.shape, 1)
-    size = sizes[lax.axis_index("sector")]
-    out[0] = jnp.where((rows < size) & (cols < size), total, 0.0).astype(BF16)
+    refs[-1][0] = total.astype(BF16)
 
 
 def shards(wavefunction, left_factors, right_factors, term_list, term_counts, sector_sizes):
@@ -121,12 +116,12 @@
     codes = pl.pallas_call(
         codes_kernel,
         out_shape=jax.ShapeDtypeStruct(term_list.shape, jnp.int32),
-        in_specs=[SMEM, SMEM],
-        out_specs=SMEM,
+        in_specs=[VMEM, VMEM],
+        out_specs=VMEM,
         compiler_params=pltpu.CompilerParams(vmem_limit_bytes=2**20),
         cost_estimate=pl.CostEstimate(flops=10**9, transcendentals=0, bytes_accessed=4 * 2**20),
         name="codes",
-    )(hbm(term_list), term_counts)
+    )(hbm(term_list), term_counts[:, None])
     friend_codes = lax.ppermute(codes, "sector", friends)
     other_codes = lax.ppermute(codes, "sector", others)
     near = pl.pallas_call(
@@ -166,11 +161,11 @@
     return pl.pallas_call(
         last_kernel,
         out_shape=jax.ShapeDtypeStruct((1, share, width), BF16),
-        in_specs=[SMEM, VMEM] + [VMEM] * len(got),
+        in_specs=[VMEM] * (1 + len(got)),
         out_specs=VMEM,
         compiler_params=PARAMS,
         name="last",
-    )(sector_sizes, kept, *got)
+    )(kept, *got)
 
 
 def solution(mesh):

time: 27.5 us -> 26.4 us (0.960)
  the two profiles are of different devices: /device:TPU:22 before, /device:TPU:2 now
where the time goes in v2:
time: 26.4 us; the launch traced here: 26.3 us
  waiting for transfers between devices  11.7 us (44%)
  Pallas kernels  8.05 us (30%)
  starting transfers between devices  5.75 us (22%)
  between operations  0.78 us (3%)
    ppermute x1, waiting for transfers between devices, shards(): other_codes = lax.ppermute(codes, 'sector', others)  7.85 us
    pallas_call x2, Pallas kernels, far(): pl.pallas_call(functools.partial(far_kernel, mine), out_shape=jax.ShapeDt...  5.23 us
    ppermute x1, waiting for transfers between devices, shards(): got = [lax.ppermute(theirs, 'group', hops[0])]  3.83 us
    ppermute x1, starting transfers between devices, shards(): other_codes = lax.ppermute(codes, 'sector', others)  2.11 us
    ppermute x1, starting transfers between devices, shards(): other_block = lax.ppermute(wavefunction, 'sector', others)  1.91 us
    ppermute x1, starting transfers between devices, shards(): friend_codes = lax.ppermute(codes, 'sector', friends)  1.65 us
    pallas_call x1, Pallas kernels, shards(): pl.pallas_call(near_kernel, out_shape=jax.ShapeDtypeStruct((width, width)...  1.17 us
    pallas_call x1, Pallas kernels, shards(): pl.pallas_call(codes_kernel, out_shape=jax.ShapeDtypeStruct(term_list.sha...  0.9 us
  transfers between devices with their start and end apart: 5, of which 2 were waited for; matrix products, arithmetic and copies ran while one was open for 0% of the time, Pallas kernels for 17%

profile of v2, /device:TPU:2, one launch (start us, length us, event | category | flops | bytes accessed | tf_op | source)
XLA Modules:
  0.0 26.3 jit_solution(15767676576083081821)
XLA Ops:
  0.0 0.0 collective-permute-start.3
  0.0 1.9 %collective-permute-start.1 = (bf16[1,512,512]{2,1,0:T(8,128)(2,1)}, bf16[1,512,512]{2,1,0:T(8,128)(2,1)S(1)}, u32[]{:S(2)}, u32[]{:S(2)}) collective-permute-start(bf16[1,512,512]{2,1,0:T(8,128)(2,1)} %own_block.1), channel_id=1, source_target_pairs={{1,2},{2,1},{3,4},{4,3},{5,6},{6,5},{7,8},{8,7},{9,10},{10,9},{11,... | collective-permute-start | bytes 1572872 | tf_op jit(solution)/shard_map/ppermute | solution.py:114
  2.6 0.0 copy-start
  2.6 0.0 copy-start.1
  2.6 0.0 copy-start.2
  2.6 0.0 copy-start.3
  2.6 0.9 %codes.1.own_codes = s32[4,3]{1,0:T(4,128)S(1)} custom-call(s32[4,3]{1,0:T(4,128)} %term_list.1, s32[1,1]{1,0:T(1,128)} %bitcast.1.term_counts), custom_call_target="tpu_custom_call" | custom-call | flops 1000000000 | bytes 4194304 | tf_op jit(solution)/shard_map/codes/pallas_call | solution.py:116
  3.5 1.7 %collective-permute-start.2 = (s32[4,3]{1,0:T(4,128)S(1)}, s32[4,3]{1,0:T(4,128)S(1)}, u32[]{:S(2)}, u32[]{:S(2)}) collective-permute-start(s32[4,3]{1,0:T(4,128)S(1)} %codes.1.own_codes), channel_id=1, source_target_pairs={{0,1},{1,0},{2,3},{3,2},{4,5},{5,4},{6,7},{7,6},{8,9},{9,8},{10,11... | collective-permute-start | bytes 152 | tf_op jit(solution)/shard_map/ppermute | solution.py:125
  5.2 2.1 %collective-permute-start = (s32[4,3]{1,0:T(4,128)S(1)}, s32[4,3]{1,0:T(4,128)S(1)}, u32[]{:S(2)}, u32[]{:S(2)}) collective-permute-start(s32[4,3]{1,0:T(4,128)S(1)} %codes.1.own_codes), channel_id=1, source_target_pairs={{1,2},{2,1},{3,4},{4,3},{5,6},{6,5},{7,8},{8,7},{9,10},{10,9},{11,... | collective-permute-start | bytes 152 | tf_op jit(solution)/shard_map/ppermute | solution.py:126
  7.3 0.0 collective-permute-done.2.friend_codes
  7.3 0.0 collective-permute-done.3.friend_block
  7.3 0.0 copy-done
  7.3 0.0 copy-done.1
  7.3 0.0 copy-done.2
  7.3 0.0 copy-done.3
  7.3 1.2 %near.1 = f32[512,512]{1,0:T(8,128)S(1)} custom-call(s32[4,3]{1,0:T(4,128)S(1)} %codes.1.own_codes, s32[4,3]{1,0:T(4,128)S(1)} %collective-permute-done.2.friend_codes, s32[16]{0:T(128)S(1)} %copy-done.3, bf16[1,512,512]{2,1,0:T(8,128)(2,1)S(1)} %copy-done.2, bf16[1,512,512]{2,1,0:T(8,128)(2,1)S(1)} %collective-permute-done.3.friend_block, ...), custom_call_target="tpu_custom_call" | custom-call | tf_op jit(solution)/shard_map/near/pallas_call | solution.py:127
  8.5 7.8 %collective-permute-done.other_codes = s32[4,3]{1,0:T(4,128)S(1)} collective-permute-done((s32[4,3]{1,0:T(4,128)S(1)}, s32[4,3]{1,0:T(4,128)S(1)}, u32[]{:S(2)}, u32[]{:S(2)}) %collective-permute-start) | collective-permute-done | bytes 80 | tf_op jit(solution)/shard_map/ppermute | solution.py:126
  16.4 0.0 collective-permute-done.1.other_block
  16.4 2.7 %far_theirs.1 = bf16[256,512]{1,0:T(8,128)(2,1)S(1)} custom-call(s32[4,3]{1,0:T(4,128)S(1)} %codes.1.own_codes, s32[4,3]{1,0:T(4,128)S(1)} %collective-permute-done.other_codes, s32[16]{0:T(128)S(1)} %copy-done.3, bf16[1,512,512]{2,1,0:T(8,128)(2,1)S(1)} %collective-permute-done.1.other_block, bf16[3,512,512]{2,1,0:T(8,128)(2,1)S(1)} %copy-done, ...), custom_call_target="tpu_custom_call" | custom-call | tf_op jit(solution)/shard_map/far_theirs/pallas_call | solution.py:138
  19.1 0.1 collective-permute-start.4
  19.2 2.5 %far_mine.1.kept = f32[256,512]{1,0:T(8,128)S(1)} custom-call(s32[4,3]{1,0:T(4,128)S(1)} %codes.1.own_codes, s32[4,3]{1,0:T(4,128)S(1)} %collective-permute-done.other_codes, s32[16]{0:T(128)S(1)} %copy-done.3, bf16[1,512,512]{2,1,0:T(8,128)(2,1)S(1)} %collective-permute-done.1.other_block, bf16[3,512,512]{2,1,0:T(8,128)(2,1)S(1)} %copy-done, ...), custom_call_target="tpu_custom_call" | custom-call | tf_op jit(solution)/shard_map/far_mine/pallas_call | solution.py:138
  21.7 3.8 %collective-permute-done.4.refs_0_ = bf16[256,512]{1,0:T(8,128)(2,1)S(1)} collective-permute-done((bf16[256,512]{1,0:T(8,128)(2,1)S(1)}, bf16[256,512]{1,0:T(8,128)(2,1)S(1)}, u32[]{:S(2)}, u32[]{:S(2)}) %collective-permute-start.4) | collective-permute-done | bytes 262176 | tf_op jit(solution)/shard_map/ppermute | solution.py:151
  25.5 0.7 %last.1 = bf16[1,256,512]{2,1,0:T(8,128)(2,1)} custom-call(f32[256,512]{1,0:T(8,128)S(1)} %far_mine.1.kept, bf16[256,512]{1,0:T(8,128)(2,1)S(1)} %collective-permute-done.4.refs_0_), custom_call_target="tpu_custom_call" | custom-call | tf_op jit(solution)/shard_map/last/pallas_call | solution.py:161
Async XLA Ops:
  0.0 7.3 %collective-permute-start.3 = (bf16[1,512,512]{2,1,0:T(8,128)(2,1)}, bf16[1,512,512]{2,1,0:T(8,128)(2,1)S(1)}, u32[]{:S(2)}, u32[]{:S(2)}) collective-permute-start(bf16[1,512,512]{2,1,0:T(8,128)(2,1)} %own_block.1), channel_id=1, source_target_pairs={{0,1},{1,0},{2,3},{3,2},{4,5},{5,4},{6,7},{7,6},{8,9},{9,8},{10,11... | collective-permute-start | bytes 1572872 | tf_op jit(solution)/shard_map/ppermute | solution.py:115
  0.0 16.4 %collective-permute-start.1 = (bf16[1,512,512]{2,1,0:T(8,128)(2,1)}, bf16[1,512,512]{2,1,0:T(8,128)(2,1)S(1)}, u32[]{:S(2)}, u32[]{:S(2)}) collective-permute-start(bf16[1,512,512]{2,1,0:T(8,128)(2,1)} %own_block.1), channel_id=1, source_target_pairs={{1,2},{2,1},{3,4},{4,3},{5,6},{6,5},{7,8},{8,7},{9,10},{10,9},{11,... | collective-permute-start | bytes 1572872 | tf_op jit(solution)/shard_map/ppermute | solution.py:114
  2.6 4.7 %copy-start = (bf16[3,512,512]{2,1,0:T(8,128)(2,1)S(1)}, bf16[3,512,512]{2,1,0:T(8,128)(2,1)}, u32[]{:S(2)}) copy-start(bf16[3,512,512]{2,1,0:T(8,128)(2,1)} %left.5) | copy-start | bytes 4718596
  2.6 4.7 %copy-start.1 = (bf16[3,512,512]{2,1,0:T(8,128)(2,1)S(1)}, bf16[3,512,512]{2,1,0:T(8,128)(2,1)}, u32[]{:S(2)}) copy-start(bf16[3,512,512]{2,1,0:T(8,128)(2,1)} %right.5) | copy-start | bytes 4718596
  2.6 4.7 %copy-start.2 = (bf16[1,512,512]{2,1,0:T(8,128)(2,1)S(1)}, bf16[1,512,512]{2,1,0:T(8,128)(2,1)}, u32[]{:S(2)}) copy-start(bf16[1,512,512]{2,1,0:T(8,128)(2,1)} %own_block.1) | copy-start | bytes 1572868
  2.6 4.7 %copy-start.3 = (s32[16]{0:T(128)S(1)}, s32[16]{0:T(128)}, u32[]{:S(2)}) copy-start(s32[16]{0:T(128)} %sizes.5) | copy-start | bytes 196
  3.5 3.8 %collective-permute-start.2 = (s32[4,3]{1,0:T(4,128)S(1)}, s32[4,3]{1,0:T(4,128)S(1)}, u32[]{:S(2)}, u32[]{:S(2)}) collective-permute-start(s32[4,3]{1,0:T(4,128)S(1)} %codes.1.own_codes), channel_id=1, source_target_pairs={{0,1},{1,0},{2,3},{3,2},{4,5},{5,4},{6,7},{7,6},{8,9},{9,8},{10,11... | collective-permute-start | bytes 152 | tf_op jit(solution)/shard_map/ppermute | solution.py:125
  5.2 11.2 %collective-permute-start = (s32[4,3]{1,0:T(4,128)S(1)}, s32[4,3]{1,0:T(4,128)S(1)}, u32[]{:S(2)}, u32[]{:S(2)}) collective-permute-start(s32[4,3]{1,0:T(4,128)S(1)} %codes.1.own_codes), channel_id=1, source_target_pairs={{1,2},{2,1},{3,4},{4,3},{5,6},{6,5},{7,8},{8,7},{9,10},{10,9},{11,... | collective-permute-start | bytes 152 | tf_op jit(solution)/shard_map/ppermute | solution.py:126
  19.1 6.4 %collective-permute-start.4 = (bf16[256,512]{1,0:T(8,128)(2,1)S(1)}, bf16[256,512]{1,0:T(8,128)(2,1)S(1)}, u32[]{:S(2)}, u32[]{:S(2)}) collective-permute-start(bf16[256,512]{1,0:T(8,128)(2,1)S(1)} %far_theirs.1), channel_id=1, source_target_pairs={{0,16},{16,0},{1,17},{17,1},{2,18},{18,2},{3,19},{19,3},{4,20},{20... | collective-permute-start | bytes 786440 | tf_op jit(solution)/shard_map/ppermute | solution.py:151

commit v3 on v2

--- a/solution.py
+++ b/solution.py
@@ -11,7 +11,7 @@
 BF16 = jnp.bfloat16
 VMEM = pl.BlockSpec(memory_space=pltpu.VMEM)
 SMEM = pl.BlockSpec(memory_space=pltpu.SMEM)
-PARAMS = pltpu.CompilerParams(vmem_limit_bytes=16 * 1024 * 1024)
+PARAMS = pltpu.CompilerParams(vmem_limit_bytes=24 * 1024 * 1024)
 
 
 def dot(a, b, ca, cb):
@@ -70,34 +70,58 @@
     live_terms(friend_codes, friend, here, lambda l, r: forward(acc, left.at[l], friend_clean, right.at[r]))
 
 
-def far_kernel(mine, own_codes, other_codes, sizes, other_block, left, right, near, out, clean, acc):
+def prep_kernel(own_codes, other_codes, sizes, left, right, plan, lhs, rhs, count):
     here = lax.axis_index("sector")
     other = other_of(here)
-    share = out.shape[0]
-    clean[...] = masked(other_block[0], sizes[jnp.clip(other, 0, sizes.shape[0] - 1)])
-
-    def run(rows):
-        first = rows.start or 0
+    size = sizes[jnp.clip(other, 0, sizes.shape[0] - 1)]
+    shape = lhs.shape[1:]
+    inside_cols = lax.broadcasted_iota(jnp.int32, shape, 1) < size
+    inside_rows = lax.broadcasted_iota(jnp.int32, shape, 0) < size
+    count[0] = 0
+
+    def add(a, b):
+        i = count[0]
+        lhs[i] = jnp.where(inside_cols, a, jnp.zeros_like(a))
+        rhs[i] = jnp.where(inside_rows, b, jnp.zeros_like(b))
+        count[0] = i + 1
+
+    live_terms(own_codes, here, other, lambda l, r: add(left[l].T, right[r].T))
+    live_terms(other_codes, other, here, lambda l, r: add(left[l], right[r]))
+    plan[...] = jnp.where(lax.broadcasted_iota(jnp.int32, plan.shape, 1) == 0, count[0], sizes[here])
+
+
+def far_kernel(groups, hops, plan, block, lhs, rhs, near, out, acc):
+    share, width = acc.shape
+    live, size = plan[0, 0], plan[0, 1]
+
+    def terms(i, n, rows):
+        a = lhs[pl.ds(i, n), rows, :].reshape(n * share, width)
+        middle = dot(a, block[0], 1, 0).astype(BF16)
+        middle = jnp.concatenate([middle[j * share:(j + 1) * share] for j in range(n)], axis=1)
+        acc[...] += dot(middle, rhs[pl.ds(i, n)].reshape(n * width, width), 1, 0)
+
+    for j, hop in enumerate(hops):
+        first = pl.multiple_of((lax.axis_index("group") + hop) % groups * share, share)
+        rows = pl.ds(first, share)
         acc[...] = near[rows, :]
-        live_terms(own_codes, here, other,
-                   lambda l, r: adjoint(acc, left.at[l, :, rows], clean, right.at[r]))
-        live_terms(other_codes, other, here,
-                   lambda l, r: forward(acc, left.at[l, rows, :], clean, right.at[r]))
-        out[...] = masked(acc[...], sizes[here], first).astype(out.dtype)
-
-    if share == near.shape[0]:
-        run(slice(None))
-        return
-    for g in range(near.shape[0] // share):
-        @pl.when((lax.axis_index("group") == g) == mine)
+
+        def pair(i, carry):
+            terms(2 * i, 2, rows)
+            return carry
+
+        lax.fori_loop(0, live // 2, pair, 0)
+
+        @pl.when(live % 2 == 1)
         def _():
-            run(slice(g * share, (g + 1) * share))
+            terms(live - 1, 1, rows)
+
+        out[j] = masked(acc[...], size, first).astype(out.dtype)
 
 
 def last_kernel(kept, *refs):
-    total = kept[...]
+    total = kept[0]
     for part in refs[:-1]:
-        total = total + part[...].astype(F32)
+        total = total + part[0].astype(F32)
     refs[-1][0] = total.astype(BF16)
 
 
@@ -119,7 +143,7 @@
         in_specs=[VMEM, VMEM],
         out_specs=VMEM,
         compiler_params=pltpu.CompilerParams(vmem_limit_bytes=2**20),
-        cost_estimate=pl.CostEstimate(flops=10**9, transcendentals=0, bytes_accessed=4 * 2**20),
+        cost_estimate=pl.CostEstimate(flops=4 * 10**9, transcendentals=0, bytes_accessed=4 * 2**22),
         name="codes",
     )(hbm(term_list), term_counts[:, None])
     friend_codes = lax.ppermute(codes, "sector", friends)
@@ -134,30 +158,38 @@
         name="near",
     )(codes, friend_codes, sector_sizes, wavefunction, friend_block, left_factors, right_factors)
 
-    def far(rows, mine, dtype):
+    terms = 2 * term_list.shape[0]
+    plan, lhs, rhs = pl.pallas_call(
+        prep_kernel,
+        out_shape=[
+            jax.ShapeDtypeStruct((1, 2), jnp.int32),
+            jax.ShapeDtypeStruct((terms, width, width), BF16),
+            jax.ShapeDtypeStruct((terms, width, width), BF16),
+        ],
+        in_specs=[SMEM, SMEM, SMEM, VMEM, VMEM],
+        out_specs=[VMEM, VMEM, VMEM],
+        scratch_shapes=[pltpu.SMEM((1,), jnp.int32)],
+        compiler_params=PARAMS,
+        name="prep",
+    )(codes, other_codes, sector_sizes, left_factors, right_factors)
+
+    def far(hops, dtype):
         return pl.pallas_call(
-            functools.partial(far_kernel, mine),
-            out_shape=jax.ShapeDtypeStruct((rows, width), dtype),
-            in_specs=[SMEM, SMEM, SMEM, VMEM, VMEM, VMEM, VMEM],
+            functools.partial(far_kernel, groups, hops),
+            out_shape=jax.ShapeDtypeStruct((len(hops), share, width), dtype),
+            in_specs=[SMEM, VMEM, VMEM, VMEM, VMEM],
             out_specs=VMEM,
-            scratch_shapes=[block, pltpu.VMEM((rows, width), F32)],
+            scratch_shapes=[pltpu.VMEM((share, width), F32)],
             compiler_params=PARAMS,
-            name="far_mine" if mine else "far_theirs",
-        )(codes, other_codes, sector_sizes, other_block, left_factors, right_factors, near)
-
-    hops = [[(g, (g + hop) % groups) for g in range(groups)] for hop in range(1, groups)]
-    if groups == 2 and share % 128 == 0:
-        theirs = far(share, False, BF16)
-        got = [lax.ppermute(theirs, "group", hops[0])]
-        kept = far(share, True, F32)
-    else:
-        whole = far(width, True, F32)
-        group = lax.axis_index("group")
-        kept = lax.dynamic_slice_in_dim(whole, group * share, share, 0)
-        got = []
-        for hop, pairs in enumerate(hops, 1):
-            part = lax.dynamic_slice_in_dim(whole, (group + hop) % groups * share, share, 0)
-            got.append(lax.ppermute(part.astype(BF16), "group", pairs))
+        )(plan, other_block, lhs, rhs, near)
+
+    hops = range(1, groups)
+    got = []
+    if groups > 1:
+        theirs = far(hops, BF16)
+        for j, hop in enumerate(hops):
+            got.append(lax.ppermute(theirs[j:j + 1], "group", [(g, (g + hop) % groups) for g in range(groups)]))
+    kept = far((0,), F32)
     return pl.pallas_call(
         last_kernel,
         out_shape=jax.ShapeDtypeStruct((1, share, width), BF16),

time: 26.4 us -> 30.1 us (1.14)
  the two profiles are of different devices: /device:TPU:2 before, /device:TPU:1 now
where the time goes in v3:
time: 30.1 us; the launch traced here: 29.9 us
  Pallas kernels  10.8 us (36%)
  waiting for transfers between devices  10.2 us (34%)
  starting transfers between devices  8.12 us (27%)
  between operations  0.77 us (3%)
    ppermute x1, waiting for transfers between devices, shards(): other_codes = lax.ppermute(codes, 'sector', others)  6.9 us
    ppermute x1, starting transfers between devices, shards(): other_block = lax.ppermute(wavefunction, 'sector', others)  4.47 us
    pallas_call x1, Pallas kernels, shards(): pl.pallas_call(near_kernel, out_shape=jax.ShapeDtypeStruct((width, width)...  3.87 us
    pallas_call x2, Pallas kernels, far(): pl.pallas_call(functools.partial(far_kernel, groups, hops), out_shape=jax...  3.74 us
    ppermute x1, starting transfers between devices, shards(): other_codes = lax.ppermute(codes, 'sector', others)  3.56 us
    ppermute x1, waiting for transfers between devices, shards(): lax.ppermute(theirs[j:j + 1], 'group', [(g, (g + hop) % groups) for g in...  3.33 us
    pallas_call x1, Pallas kernels, shards(): pl.pallas_call(prep_kernel, out_shape=[jax.ShapeDtypeStruct((1, 2), jnp.i...  1.47 us
    pallas_call x1, Pallas kernels, shards(): pl.pallas_call(codes_kernel, out_shape=jax.ShapeDtypeStruct(term_list.sha...  0.9 us
  transfers between devices with their start and end apart: 5, of which 2 were waited for; matrix products, arithmetic and copies ran while one was open for 0% of the time, Pallas kernels for 27%

profile of v3, /device:TPU:1, one launch (start us, length us, event | category | flops | bytes accessed | tf_op | source)
XLA Modules:
  0.0 29.9 jit_solution(12489795464175110144)
XLA Ops:
  0.0 0.0 collective-permute-start.3
  0.0 4.5 %collective-permute-start.1 = (bf16[1,512,512]{2,1,0:T(8,128)(2,1)}, bf16[1,512,512]{2,1,0:T(8,128)(2,1)S(1)}, u32[]{:S(2)}, u32[]{:S(2)}) collective-permute-start(bf16[1,512,512]{2,1,0:T(8,128)(2,1)} %own_block.1), channel_id=1, source_target_pairs={{1,2},{2,1},{3,4},{4,3},{5,6},{6,5},{7,8},{8,7},{9,10},{10,9},{11,... | collective-permute-start | bytes 1572872 | tf_op jit(solution)/shard_map/ppermute | solution.py:138
  5.1 0.0 copy-start
  5.2 0.0 copy-start.1
  5.2 0.0 copy-start.3
  5.2 0.0 copy-start.2
  5.2 0.9 %codes.1.own_codes = s32[4,3]{1,0:T(4,128)S(1)} custom-call(s32[4,3]{1,0:T(4,128)} %term_list.1, s32[1,1]{1,0:T(1,128)} %bitcast.1.term_counts), custom_call_target="tpu_custom_call" | custom-call | flops 4000000000 | bytes 16777216 | tf_op jit(solution)/shard_map/codes/pallas_call | solution.py:140
  6.1 0.0 collective-permute-start.2
  6.1 3.6 %collective-permute-start = (s32[4,3]{1,0:T(4,128)S(1)}, s32[4,3]{1,0:T(4,128)S(1)}, u32[]{:S(2)}, u32[]{:S(2)}) collective-permute-start(s32[4,3]{1,0:T(4,128)S(1)} %codes.1.own_codes), channel_id=1, source_target_pairs={{1,2},{2,1},{3,4},{4,3},{5,6},{6,5},{7,8},{8,7},{9,10},{10,9},{11,... | collective-permute-start | bytes 152 | tf_op jit(solution)/shard_map/ppermute | solution.py:150
  9.7 6.9 %collective-permute-done.other_codes = s32[4,3]{1,0:T(4,128)S(1)} collective-permute-done((s32[4,3]{1,0:T(4,128)S(1)}, s32[4,3]{1,0:T(4,128)S(1)}, u32[]{:S(2)}, u32[]{:S(2)}) %collective-permute-start) | collective-permute-done | bytes 80 | tf_op jit(solution)/shard_map/ppermute | solution.py:150
  16.6 0.0 copy-done
  16.6 0.0 copy-done.1
  16.6 0.0 copy-done.3
  16.6 1.5 %prep.1 = (s32[1,2]{1,0:T(1,128)S(1)}, bf16[8,512,512]{2,1,0:T(8,128)(2,1)S(1)}, bf16[8,512,512]{2,1,0:T(8,128)(2,1)S(1)}) custom-call(s32[4,3]{1,0:T(4,128)S(1)} %codes.1.own_codes, s32[4,3]{1,0:T(4,128)S(1)} %collective-permute-done.other_codes, s32[16]{0:T(128)S(1)} %copy-done.3, bf16[3,512,512]{2,1,0:T(8,128)(2,1)S(1)} %copy-done, ...), custom_call_target="tpu_custom_call" | custom-call | tf_op jit(solution)/shard_map/prep/pallas_call | solution.py:162
  18.0 0.0 collective-permute-done.2.friend_codes
  18.1 0.0 collective-permute-done.3.friend_block
  18.1 0.0 copy-done.2
  18.1 3.9 %near.1 = f32[512,512]{1,0:T(8,128)S(1)} custom-call(s32[4,3]{1,0:T(4,128)S(1)} %codes.1.own_codes, s32[4,3]{1,0:T(4,128)S(1)} %collective-permute-done.2.friend_codes, s32[16]{0:T(128)S(1)} %copy-done.3, bf16[1,512,512]{2,1,0:T(8,128)(2,1)S(1)} %copy-done.2, bf16[1,512,512]{2,1,0:T(8,128)(2,1)S(1)} %collective-permute-done.3.friend_block, ...), custom_call_target="tpu_custom_call" | custom-call | tf_op jit(solution)/shard_map/near/pallas_call | solution.py:151
  22.0 0.0 collective-permute-done.1.block
  22.0 1.9 %shard_map.65 = bf16[1,256,512]{2,1,0:T(8,128)(2,1)S(1)} custom-call(s32[1,2]{1,0:T(1,128)S(1)} %get-tuple-element.8.plan, bf16[1,512,512]{2,1,0:T(8,128)(2,1)S(1)} %collective-permute-done.1.block, bf16[8,512,512]{2,1,0:T(8,128)(2,1)S(1)} %get-tuple-element.9.lhs, bf16[8,512,512]{2,1,0:T(8,128)(2,1)S(1)} %get-tuple-element.10.rhs, f32[512,512]{1,0:T(8,128)S(1)} %near.1), custom_call_target="tpu_custom_call" | custom-call | tf_op jit(solution)/shard_map/pallas_call | solution.py:177
  23.8 0.1 collective-permute-start.4
  23.9 1.9 %shard_map.64.kept = f32[1,256,512]{2,1,0:T(8,128)S(1)} custom-call(s32[1,2]{1,0:T(1,128)S(1)} %get-tuple-element.8.plan, bf16[1,512,512]{2,1,0:T(8,128)(2,1)S(1)} %collective-permute-done.1.block, bf16[8,512,512]{2,1,0:T(8,128)(2,1)S(1)} %get-tuple-element.9.lhs, bf16[8,512,512]{2,1,0:T(8,128)(2,1)S(1)} %get-tuple-element.10.rhs, f32[512,512]{1,0:T(8,128)S(1)} %near.1), custom_call_target="tpu_custom_call" | custom-call | tf_op jit(solution)/shard_map/pallas_call | solution.py:177
  25.8 3.3 %collective-permute-done.4.refs_0_ = bf16[1,256,512]{2,1,0:T(8,128)(2,1)S(1)} collective-permute-done((bf16[1,256,512]{2,1,0:T(8,128)(2,1)S(1)}, bf16[1,256,512]{2,1,0:T(8,128)(2,1)S(1)}, u32[]{:S(2)}, u32[]{:S(2)}) %collective-permute-start.4) | collective-permute-done | bytes 262176 | tf_op jit(solution)/shard_map/ppermute | solution.py:191
  29.1 0.8 %last.1 = bf16[1,256,512]{2,1,0:T(8,128)(2,1)} custom-call(f32[1,256,512]{2,1,0:T(8,128)S(1)} %shard_map.64.kept, bf16[1,256,512]{2,1,0:T(8,128)(2,1)S(1)} %collective-permute-done.4.refs_0_), custom_call_target="tpu_custom_call" | custom-call | tf_op jit(solution)/shard_map/last/pallas_call | solution.py:193
Async XLA Ops:
  0.0 18.1 %collective-permute-start.3 = (bf16[1,512,512]{2,1,0:T(8,128)(2,1)}, bf16[1,512,512]{2,1,0:T(8,128)(2,1)S(1)}, u32[]{:S(2)}, u32[]{:S(2)}) collective-permute-start(bf16[1,512,512]{2,1,0:T(8,128)(2,1)} %own_block.1), channel_id=1, source_target_pairs={{0,1},{1,0},{2,3},{3,2},{4,5},{5,4},{6,7},{7,6},{8,9},{9,8},{10,11... | collective-permute-start | bytes 1572872 | tf_op jit(solution)/shard_map/ppermute | solution.py:139
  0.0 21.9 %collective-permute-start.1 = (bf16[1,512,512]{2,1,0:T(8,128)(2,1)}, bf16[1,512,512]{2,1,0:T(8,128)(2,1)S(1)}, u32[]{:S(2)}, u32[]{:S(2)}) collective-permute-start(bf16[1,512,512]{2,1,0:T(8,128)(2,1)} %own_block.1), channel_id=1, source_target_pairs={{1,2},{2,1},{3,4},{4,3},{5,6},{6,5},{7,8},{8,7},{9,10},{10,9},{11,... | collective-permute-start | bytes 1572872 | tf_op jit(solution)/shard_map/ppermute | solution.py:138
  5.1 11.4 %copy-start = (bf16[3,512,512]{2,1,0:T(8,128)(2,1)S(1)}, bf16[3,512,512]{2,1,0:T(8,128)(2,1)}, u32[]{:S(2)}) copy-start(bf16[3,512,512]{2,1,0:T(8,128)(2,1)} %left.3) | copy-start | bytes 4718596
  5.2 11.4 %copy-start.1 = (bf16[3,512,512]{2,1,0:T(8,128)(2,1)S(1)}, bf16[3,512,512]{2,1,0:T(8,128)(2,1)}, u32[]{:S(2)}) copy-start(bf16[3,512,512]{2,1,0:T(8,128)(2,1)} %right.3) | copy-start | bytes 4718596
  5.2 11.4 %copy-start.3 = (s32[16]{0:T(128)S(1)}, s32[16]{0:T(128)}, u32[]{:S(2)}) copy-start(s32[16]{0:T(128)} %sizes.3) | copy-start | bytes 196
  5.2 12.9 %copy-start.2 = (bf16[1,512,512]{2,1,0:T(8,128)(2,1)S(1)}, bf16[1,512,512]{2,1,0:T(8,128)(2,1)}, u32[]{:S(2)}) copy-start(bf16[1,512,512]{2,1,0:T(8,128)(2,1)} %own_block.1) | copy-start | bytes 1572868
  6.1 12.0 %collective-permute-start.2 = (s32[4,3]{1,0:T(4,128)S(1)}, s32[4,3]{1,0:T(4,128)S(1)}, u32[]{:S(2)}, u32[]{:S(2)}) collective-permute-start(s32[4,3]{1,0:T(4,128)S(1)} %codes.1.own_codes), channel_id=1, source_target_pairs={{0,1},{1,0},{2,3},{3,2},{4,5},{5,4},{6,7},{7,6},{8,9},{9,8},{10,11... | collective-permute-start | bytes 152 | tf_op jit(solution)/shard_map/ppermute | solution.py:149
  6.1 10.5 %collective-permute-start = (s32[4,3]{1,0:T(4,128)S(1)}, s32[4,3]{1,0:T(4,128)S(1)}, u32[]{:S(2)}, u32[]{:S(2)}) collective-permute-start(s32[4,3]{1,0:T(4,128)S(1)} %codes.1.own_codes), channel_id=1, source_target_pairs={{1,2},{2,1},{3,4},{4,3},{5,6},{6,5},{7,8},{8,7},{9,10},{10,9},{11,... | collective-permute-start | bytes 152 | tf_op jit(solution)/shard_map/ppermute | solution.py:150
  23.8 5.3 %collective-permute-start.4 = (bf16[1,256,512]{2,1,0:T(8,128)(2,1)S(1)}, bf16[1,256,512]{2,1,0:T(8,128)(2,1)S(1)}, u32[]{:S(2)}, u32[]{:S(2)}) collective-permute-start(bf16[1,256,512]{2,1,0:T(8,128)(2,1)S(1)} %shard_map.65), channel_id=1, source_target_pairs={{0,16},{16,0},{1,17},{17,1},{2,18},{18,2},{3,19},{19,3},{4,20},{20... | collective-permute-start | bytes 786440 | tf_op jit(solution)/shard_map/ppermute | solution.py:191

commit v4 on v3

--- a/solution.py
+++ b/solution.py
@@ -70,35 +70,42 @@
     live_terms(friend_codes, friend, here, lambda l, r: forward(acc, left.at[l], friend_clean, right.at[r]))
 
 
-def prep_kernel(own_codes, other_codes, sizes, left, right, plan, lhs, rhs, count):
+def prep_kernel(sizes, left, right, lhs, rhs):
+    other = other_of(lax.axis_index("sector"))
+    size = sizes[jnp.clip(other, 0, sizes.shape[0] - 1)]
+    count, *shape = left.shape
+    inside_cols = lax.broadcasted_iota(jnp.int32, shape, 1) < size
+    inside_rows = lax.broadcasted_iota(jnp.int32, shape, 0) < size
+
+    def one(i, carry):
+        a, b = left[i], right[i]
+        lhs[i] = jnp.where(inside_cols, a, jnp.zeros_like(a))
+        rhs[i] = jnp.where(inside_rows, b, jnp.zeros_like(b))
+        lhs[count + i] = jnp.where(inside_cols, a.T, jnp.zeros_like(a))
+        rhs[count + i] = jnp.where(inside_rows, b.T, jnp.zeros_like(b))
+        return carry
+
+    lax.fori_loop(0, count, one, 0)
+
+
+def far_kernel(groups, hops, own_codes, other_codes, sizes, block, lhs, rhs, near, out, acc, left_picks, right_picks):
+    share, _ = acc.shape
     here = lax.axis_index("sector")
     other = other_of(here)
-    size = sizes[jnp.clip(other, 0, sizes.shape[0] - 1)]
-    shape = lhs.shape[1:]
-    inside_cols = lax.broadcasted_iota(jnp.int32, shape, 1) < size
-    inside_rows = lax.broadcasted_iota(jnp.int32, shape, 0) < size
-    count[0] = 0
-
-    def add(a, b):
-        i = count[0]
-        lhs[i] = jnp.where(inside_cols, a, jnp.zeros_like(a))
-        rhs[i] = jnp.where(inside_rows, b, jnp.zeros_like(b))
-        count[0] = i + 1
-
-    live_terms(own_codes, here, other, lambda l, r: add(left[l].T, right[r].T))
-    live_terms(other_codes, other, here, lambda l, r: add(left[l], right[r]))
-    plan[...] = jnp.where(lax.broadcasted_iota(jnp.int32, plan.shape, 1) == 0, count[0], sizes[here])
-
-
-def far_kernel(groups, hops, plan, block, lhs, rhs, near, out, acc):
-    share, width = acc.shape
-    live, size = plan[0, 0], plan[0, 1]
+    count = lhs.shape[0] // 2
+    live = jnp.int32(0)
+    for codes, owner, want, skip in ((own_codes, here, other, count), (other_codes, other, here, 0)):
+        for k in range(codes.shape[0]):
+            left_picks[live] = skip + codes[k, 1] - 1
+            right_picks[live] = skip + codes[k, 2] - 1
+            live += (owner + codes[k, 0] - 2 == want).astype(jnp.int32)
 
     def terms(i, n, rows):
-        a = lhs[pl.ds(i, n), rows, :].reshape(n * share, width)
+        a = jnp.concatenate([lhs[left_picks[i + j], rows, :] for j in range(n)], axis=0)
+        b = jnp.concatenate([rhs[right_picks[i + j]] for j in range(n)], axis=0)
         middle = dot(a, block[0], 1, 0).astype(BF16)
         middle = jnp.concatenate([middle[j * share:(j + 1) * share] for j in range(n)], axis=1)
-        acc[...] += dot(middle, rhs[pl.ds(i, n)].reshape(n * width, width), 1, 0)
+        acc[...] += dot(middle, b, 1, 0)
 
     for j, hop in enumerate(hops):
         first = pl.multiple_of((lax.axis_index("group") + hop) % groups * share, share)
@@ -115,7 +122,7 @@
         def _():
             terms(live - 1, 1, rows)
 
-        out[j] = masked(acc[...], size, first).astype(out.dtype)
+        out[j] = masked(acc[...], sizes[here], first).astype(out.dtype)
 
 
 def last_kernel(kept, *refs):
@@ -158,30 +165,26 @@
         name="near",
     )(codes, friend_codes, sector_sizes, wavefunction, friend_block, left_factors, right_factors)
 
-    terms = 2 * term_list.shape[0]
-    plan, lhs, rhs = pl.pallas_call(
+    laid_out = jax.ShapeDtypeStruct((2 * left_factors.shape[0], width, width), BF16)
+    lhs, rhs = pl.pallas_call(
         prep_kernel,
-        out_shape=[
-            jax.ShapeDtypeStruct((1, 2), jnp.int32),
-            jax.ShapeDtypeStruct((terms, width, width), BF16),
-            jax.ShapeDtypeStruct((terms, width, width), BF16),
-        ],
-        in_specs=[SMEM, SMEM, SMEM, VMEM, VMEM],
-        out_specs=[VMEM, VMEM, VMEM],
-        scratch_shapes=[pltpu.SMEM((1,), jnp.int32)],
+        out_shape=[laid_out, laid_out],
+        in_specs=[SMEM, VMEM, VMEM],
+        out_specs=[VMEM, VMEM],
         compiler_params=PARAMS,
         name="prep",
-    )(codes, other_codes, sector_sizes, left_factors, right_factors)
+    )(sector_sizes, left_factors, right_factors)
+    picks = pltpu.SMEM((2 * term_list.shape[0],), jnp.int32)
 
     def far(hops, dtype):
         return pl.pallas_call(
             functools.partial(far_kernel, groups, hops),
             out_shape=jax.ShapeDtypeStruct((len(hops), share, width), dtype),
-            in_specs=[SMEM, VMEM, VMEM, VMEM, VMEM],
+            in_specs=[SMEM, SMEM, SMEM, VMEM, VMEM, VMEM, VMEM],
             out_specs=VMEM,
-            scratch_shapes=[pltpu.VMEM((share, width), F32)],
+            scratch_shapes=[pltpu.VMEM((share, width), F32), picks, picks],
             compiler_params=PARAMS,
-        )(plan, other_block, lhs, rhs, near)
+        )(codes, other_codes, sector_sizes, other_block, lhs, rhs, near)
 
     hops = range(1, groups)
     got = []

time: 30.1 us -> 27.4 us (0.910)
  the two profiles are of different devices: /device:TPU:1 before, /device:TPU:23 now
where the time goes in v4:
time: 27.4 us; the launch traced here: 27.3 us
  Pallas kernels  13 us (47%)
  starting transfers between devices  7.44 us (27%)
  waiting for transfers between devices  6.06 us (22%)
  between operations  0.79 us (3%)
    ppermute x1, waiting for transfers between devices, shards(): lax.ppermute(theirs[j:j + 1], 'group', [(g, (g + hop) % groups) for g in...  6.05 us
    pallas_call x1, Pallas kernels, shards(): pl.pallas_call(near_kernel, out_shape=jax.ShapeDtypeStruct((width, width)...  5.66 us
    pallas_call x2, Pallas kernels, far(): pl.pallas_call(functools.partial(far_kernel, groups, hops), out_shape=jax...  3.93 us
    ppermute x1, starting transfers between devices, shards(): other_codes = lax.ppermute(codes, 'sector', others)  3.63 us
    ppermute x1, starting transfers between devices, shards(): other_block = lax.ppermute(wavefunction, 'sector', others)  3.05 us
    pallas_call x1, Pallas kernels, shards(): pl.pallas_call(prep_kernel, out_shape=[laid_out, laid_out], in_specs=[SME...  1.71 us
    pallas_call x1, Pallas kernels, shards(): pl.pallas_call(codes_kernel, out_shape=jax.ShapeDtypeStruct(term_list.sha...  0.9 us
    pallas_call x1, Pallas kernels, shards(): pl.pallas_call(last_kernel, out_shape=jax.ShapeDtypeStruct((1, share, wid...  0.76 us
  transfers between devices with their start and end apart: 5, of which 1 were waited for; matrix products, arithmetic and copies ran while one was open for 0% of the time, Pallas kernels for 37%

profile of v4, /device:TPU:23, one launch (start us, length us, event | category | flops | bytes accessed | tf_op | source)
XLA Modules:
  0.0 27.3 jit_solution(5784491338075297182)
XLA Ops:
  0.0 0.7 %collective-permute-start.3 = (bf16[1,512,512]{2,1,0:T(8,128)(2,1)}, bf16[1,512,512]{2,1,0:T(8,128)(2,1)S(1)}, u32[]{:S(2)}, u32[]{:S(2)}) collective-permute-start(bf16[1,512,512]{2,1,0:T(8,128)(2,1)} %own_block.1), channel_id=1, source_target_pairs={{0,1},{1,0},{2,3},{3,2},{4,5},{5,4},{6,7},{7,6},{8,9},{9,8},{10,11... | collective-permute-start | bytes 1572872 | tf_op jit(solution)/shard_map/ppermute | solution.py:146
  0.7 3.1 %collective-permute-start.1 = (bf16[1,512,512]{2,1,0:T(8,128)(2,1)}, bf16[1,512,512]{2,1,0:T(8,128)(2,1)S(1)}, u32[]{:S(2)}, u32[]{:S(2)}) collective-permute-start(bf16[1,512,512]{2,1,0:T(8,128)(2,1)} %own_block.1), channel_id=1, source_target_pairs={{1,2},{2,1},{3,4},{4,3},{5,6},{6,5},{7,8},{8,7},{9,10},{10,9},{11,... | collective-permute-start | bytes 1572872 | tf_op jit(solution)/shard_map/ppermute | solution.py:145
  4.4 0.0 copy-start
  4.4 0.0 copy-start.1
  4.4 0.0 copy-start.3
  4.4 0.9 %codes.1.own_codes = s32[4,3]{1,0:T(4,128)S(1)} custom-call(s32[4,3]{1,0:T(4,128)} %term_list.1, s32[1,1]{1,0:T(1,128)} %bitcast.1.term_counts), custom_call_target="tpu_custom_call" | custom-call | flops 4000000000 | bytes 16777216 | tf_op jit(solution)/shard_map/codes/pallas_call | solution.py:147
  5.3 0.0 copy-start.2
  5.3 0.0 collective-permute-start.2
  5.3 3.6 %collective-permute-start = (s32[4,3]{1,0:T(4,128)S(1)}, s32[4,3]{1,0:T(4,128)S(1)}, u32[]{:S(2)}, u32[]{:S(2)}) collective-permute-start(s32[4,3]{1,0:T(4,128)S(1)} %codes.1.own_codes), channel_id=1, source_target_pairs={{1,2},{2,1},{3,4},{4,3},{5,6},{6,5},{7,8},{8,7},{9,10},{10,9},{11,... | collective-permute-start | bytes 152 | tf_op jit(solution)/shard_map/ppermute | solution.py:157
  9.0 0.0 copy-done
  9.0 0.0 copy-done.1
  9.0 0.0 copy-done.3
  9.0 1.7 %prep.1 = (bf16[6,512,512]{2,1,0:T(8,128)(2,1)S(1)}, bf16[6,512,512]{2,1,0:T(8,128)(2,1)S(1)}) custom-call(s32[16]{0:T(128)S(1)} %copy-done.3, bf16[3,512,512]{2,1,0:T(8,128)(2,1)S(1)} %copy-done, bf16[3,512,512]{2,1,0:T(8,128)(2,1)S(1)} %copy-done.1), custom_call_target="tpu_custom_call" | custom-call | tf_op jit(solution)/shard_map/prep/pallas_call | solution.py:169
  10.7 0.0 collective-permute-done.2.friend_codes
  10.7 0.0 collective-permute-done.3.friend_block
  10.7 0.0 copy-done.2
  10.7 5.7 %near.1 = f32[512,512]{1,0:T(8,128)S(1)} custom-call(s32[4,3]{1,0:T(4,128)S(1)} %codes.1.own_codes, s32[4,3]{1,0:T(4,128)S(1)} %collective-permute-done.2.friend_codes, s32[16]{0:T(128)S(1)} %copy-done.3, bf16[1,512,512]{2,1,0:T(8,128)(2,1)S(1)} %copy-done.2, bf16[1,512,512]{2,1,0:T(8,128)(2,1)S(1)} %collective-permute-done.3.friend_block, ...), custom_call_target="tpu_custom_call" | custom-call | tf_op jit(solution)/shard_map/near/pallas_call | solution.py:158
  16.4 0.0 collective-permute-done.other_codes
  16.4 0.0 collective-permute-done.1.block
  16.4 2.0 %shard_map.65 = bf16[1,256,512]{2,1,0:T(8,128)(2,1)S(1)} custom-call(s32[4,3]{1,0:T(4,128)S(1)} %codes.1.own_codes, s32[4,3]{1,0:T(4,128)S(1)} %collective-permute-done.other_codes, s32[16]{0:T(128)S(1)} %copy-done.3, bf16[1,512,512]{2,1,0:T(8,128)(2,1)S(1)} %collective-permute-done.1.block, bf16[6,512,512]{2,1,0:T(8,128)(2,1)S(1)} %get-tuple-element.7.lhs, ...), custom_call_target="tpu_custom_call" | custom-call | tf_op jit(solution)/shard_map/pallas_call | solution.py:180
  18.4 0.1 collective-permute-start.4
  18.5 2.0 %shard_map.64.kept = f32[1,256,512]{2,1,0:T(8,128)S(1)} custom-call(s32[4,3]{1,0:T(4,128)S(1)} %codes.1.own_codes, s32[4,3]{1,0:T(4,128)S(1)} %collective-permute-done.other_codes, s32[16]{0:T(128)S(1)} %copy-done.3, bf16[1,512,512]{2,1,0:T(8,128)(2,1)S(1)} %collective-permute-done.1.block, bf16[6,512,512]{2,1,0:T(8,128)(2,1)S(1)} %get-tuple-element.7.lhs, ...), custom_call_target="tpu_custom_call" | custom-call | tf_op jit(solution)/shard_map/pallas_call | solution.py:180
  20.5 6.1 %collective-permute-done.4.refs_0_ = bf16[1,256,512]{2,1,0:T(8,128)(2,1)S(1)} collective-permute-done((bf16[1,256,512]{2,1,0:T(8,128)(2,1)S(1)}, bf16[1,256,512]{2,1,0:T(8,128)(2,1)S(1)}, u32[]{:S(2)}, u32[]{:S(2)}) %collective-permute-start.4) | collective-permute-done | bytes 262176 | tf_op jit(solution)/shard_map/ppermute | solution.py:194
  26.5 0.8 %last.1 = bf16[1,256,512]{2,1,0:T(8,128)(2,1)} custom-call(f32[1,256,512]{2,1,0:T(8,128)S(1)} %shard_map.64.kept, bf16[1,256,512]{2,1,0:T(8,128)(2,1)S(1)} %collective-permute-done.4.refs_0_), custom_call_target="tpu_custom_call" | custom-call | tf_op jit(solution)/shard_map/last/pallas_call | solution.py:196
Async XLA Ops:
  0.0 10.7 %collective-permute-start.3 = (bf16[1,512,512]{2,1,0:T(8,128)(2,1)}, bf16[1,512,512]{2,1,0:T(8,128)(2,1)S(1)}, u32[]{:S(2)}, u32[]{:S(2)}) collective-permute-start(bf16[1,512,512]{2,1,0:T(8,128)(2,1)} %own_block.1), channel_id=1, source_target_pairs={{0,1},{1,0},{2,3},{3,2},{4,5},{5,4},{6,7},{7,6},{8,9},{9,8},{10,11... | collective-permute-start | bytes 1572872 | tf_op jit(solution)/shard_map/ppermute | solution.py:146
  0.7 15.7 %collective-permute-start.1 = (bf16[1,512,512]{2,1,0:T(8,128)(2,1)}, bf16[1,512,512]{2,1,0:T(8,128)(2,1)S(1)}, u32[]{:S(2)}, u32[]{:S(2)}) collective-permute-start(bf16[1,512,512]{2,1,0:T(8,128)(2,1)} %own_block.1), channel_id=1, source_target_pairs={{1,2},{2,1},{3,4},{4,3},{5,6},{6,5},{7,8},{8,7},{9,10},{10,9},{11,... | collective-permute-start | bytes 1572872 | tf_op jit(solution)/shard_map/ppermute | solution.py:145
  4.4 4.6 %copy-start = (bf16[3,512,512]{2,1,0:T(8,128)(2,1)S(1)}, bf16[3,512,512]{2,1,0:T(8,128)(2,1)}, u32[]{:S(2)}) copy-start(bf16[3,512,512]{2,1,0:T(8,128)(2,1)} %left.3) | copy-start | bytes 4718596
  4.4 4.6 %copy-start.1 = (bf16[3,512,512]{2,1,0:T(8,128)(2,1)S(1)}, bf16[3,512,512]{2,1,0:T(8,128)(2,1)}, u32[]{:S(2)}) copy-start(bf16[3,512,512]{2,1,0:T(8,128)(2,1)} %right.3) | copy-start | bytes 4718596
  4.4 4.6 %copy-start.3 = (s32[16]{0:T(128)S(1)}, s32[16]{0:T(128)}, u32[]{:S(2)}) copy-start(s32[16]{0:T(128)} %sizes.7) | copy-start | bytes 196
  5.3 5.4 %copy-start.2 = (bf16[1,512,512]{2,1,0:T(8,128)(2,1)S(1)}, bf16[1,512,512]{2,1,0:T(8,128)(2,1)}, u32[]{:S(2)}) copy-start(bf16[1,512,512]{2,1,0:T(8,128)(2,1)} %own_block.1) | copy-start | bytes 1572868
  5.3 5.4 %collective-permute-start.2 = (s32[4,3]{1,0:T(4,128)S(1)}, s32[4,3]{1,0:T(4,128)S(1)}, u32[]{:S(2)}, u32[]{:S(2)}) collective-permute-start(s32[4,3]{1,0:T(4,128)S(1)} %codes.1.own_codes), channel_id=1, source_target_pairs={{0,1},{1,0},{2,3},{3,2},{4,5},{5,4},{6,7},{7,6},{8,9},{9,8},{10,11... | collective-permute-start | bytes 152 | tf_op jit(solution)/shard_map/ppermute | solution.py:156
  5.3 11.1 %collective-permute-start = (s32[4,3]{1,0:T(4,128)S(1)}, s32[4,3]{1,0:T(4,128)S(1)}, u32[]{:S(2)}, u32[]{:S(2)}) collective-permute-start(s32[4,3]{1,0:T(4,128)S(1)} %codes.1.own_codes), channel_id=1, source_target_pairs={{1,2},{2,1},{3,4},{4,3},{5,6},{6,5},{7,8},{8,7},{9,10},{10,9},{11,... | collective-permute-start | bytes 152 | tf_op jit(solution)/shard_map/ppermute | solution.py:157
  18.4 8.1 %collective-permute-start.4 = (bf16[1,256,512]{2,1,0:T(8,128)(2,1)S(1)}, bf16[1,256,512]{2,1,0:T(8,128)(2,1)S(1)}, u32[]{:S(2)}, u32[]{:S(2)}) collective-permute-start(bf16[1,256,512]{2,1,0:T(8,128)(2,1)S(1)} %shard_map.65), channel_id=1, source_target_pairs={{0,16},{16,0},{1,17},{17,1},{2,18},{18,2},{3,19},{19,3},{4,20},{20... | collective-permute-start | bytes 786440 | tf_op jit(solution)/shard_map/ppermute | solution.py:194

commit v5 on v2

--- a/solution.py
+++ b/solution.py
@@ -42,6 +42,12 @@
     return jnp.where((rows < size) & (cols < size), block, jnp.zeros_like(block))
 
 
+def cleaned(block, size):
+    rows = lax.broadcasted_iota(jnp.int32, (block.shape[0], 1), 0) < size
+    cols = lax.broadcasted_iota(jnp.int32, (1, block.shape[1]), 1) < size
+    return block * rows.astype(BF16) * cols.astype(BF16)
+
+
 def live_terms(codes, owner, want, action):
     for k in range(codes.shape[0]):
         @pl.when(owner + codes[k, 0] - 2 == want)
@@ -57,8 +63,8 @@
 def near_kernel(own_codes, friend_codes, sizes, own_block, friend_block, left, right, acc, clean, friend_clean):
     here = lax.axis_index("sector")
     friend = friend_of(here)
-    clean[...] = masked(own_block[0], sizes[here])
-    friend_clean[...] = masked(friend_block[0], sizes[jnp.minimum(friend, sizes.shape[0] - 1)])
+    clean[...] = cleaned(own_block[0], sizes[here])
+    friend_clean[...] = cleaned(friend_block[0], sizes[jnp.minimum(friend, sizes.shape[0] - 1)])
     acc[...] = jnp.zeros_like(acc)
 
     def self_term(l, r):
@@ -70,19 +76,59 @@
     live_terms(friend_codes, friend, here, lambda l, r: forward(acc, left.at[l], friend_clean, right.at[r]))
 
 
-def far_kernel(mine, own_codes, other_codes, sizes, other_block, left, right, near, out, clean, acc):
+def picked(codes, owner, want, lefts, rights):
+    live = jnp.int32(0)
+    for k in range(codes.shape[0]):
+        lefts[live] = codes[k, 1] - 1
+        rights[live] = codes[k, 2] - 1
+        live += (owner + codes[k, 0] - 2 == want).astype(jnp.int32)
+    return live
+
+
+def in_pairs(live, terms):
+    def pair(i, carry):
+        terms(2 * i, 2)
+        return carry
+
+    lax.fori_loop(0, live // 2, pair, 0)
+
+    @pl.when(live % 2 == 1)
+    def _():
+        terms(live - 1, 1)
+
+
+def side_by_side(stacked, n):
+    rows = stacked.shape[0] // n
+    return jnp.concatenate([stacked[j * rows:(j + 1) * rows] for j in range(n)], axis=1)
+
+
+def far_kernel(mine, own_codes, other_codes, sizes, other_block, left, right, near, out, clean, acc,
+               own_left, own_right, other_left, other_right):
     here = lax.axis_index("sector")
     other = other_of(here)
     share = out.shape[0]
-    clean[...] = masked(other_block[0], sizes[jnp.clip(other, 0, sizes.shape[0] - 1)])
+    clean[...] = cleaned(other_block[0], sizes[jnp.clip(other, 0, sizes.shape[0] - 1)])
+    adjoints = picked(own_codes, here, other, own_left, own_right)
+    forwards = picked(other_codes, other, here, other_left, other_right)
 
     def run(rows):
         first = rows.start or 0
         acc[...] = near[rows, :]
-        live_terms(own_codes, here, other,
-                   lambda l, r: adjoint(acc, left.at[l, :, rows], clean, right.at[r]))
-        live_terms(other_codes, other, here,
-                   lambda l, r: forward(acc, left.at[l, rows, :], clean, right.at[r]))
+
+        def forward_terms(i, n):
+            lefts = jnp.concatenate([left[other_left[i + j], rows, :] for j in range(n)], axis=0)
+            rights = jnp.concatenate([right[other_right[i + j]] for j in range(n)], axis=0)
+            middle = dot(lefts, clean[...], 1, 0).astype(BF16)
+            acc[...] += dot(side_by_side(middle, n), rights, 1, 0)
+
+        def adjoint_terms(i, n):
+            lefts = jnp.concatenate([left[own_left[i + j], :, rows] for j in range(n)], axis=1)
+            rights = jnp.concatenate([right[own_right[i + j]] for j in range(n)], axis=1)
+            middle = dot(lefts, clean[...], 0, 0).astype(BF16)
+            acc[...] += dot(side_by_side(middle, n), rights, 1, 1)
+
+        in_pairs(forwards, forward_terms)
+        in_pairs(adjoints, adjoint_terms)
         out[...] = masked(acc[...], sizes[here], first).astype(out.dtype)
 
     if share == near.shape[0]:
@@ -119,7 +165,7 @@
         in_specs=[VMEM, VMEM],
         out_specs=VMEM,
         compiler_params=pltpu.CompilerParams(vmem_limit_bytes=2**20),
-        cost_estimate=pl.CostEstimate(flops=10**9, transcendentals=0, bytes_accessed=4 * 2**20),
+        cost_estimate=pl.CostEstimate(flops=4 * 10**9, transcendentals=0, bytes_accessed=2**24),
         name="codes",
     )(hbm(term_list), term_counts[:, None])
     friend_codes = lax.ppermute(codes, "sector", friends)
@@ -134,13 +180,15 @@
         name="near",
     )(codes, friend_codes, sector_sizes, wavefunction, friend_block, left_factors, right_factors)
 
+    picks = pltpu.SMEM((term_list.shape[0],), jnp.int32)
+
     def far(rows, mine, dtype):
         return pl.pallas_call(
             functools.partial(far_kernel, mine),
             out_shape=jax.ShapeDtypeStruct((rows, width), dtype),
             in_specs=[SMEM, SMEM, SMEM, VMEM, VMEM, VMEM, VMEM],
             out_specs=VMEM,
-            scratch_shapes=[block, pltpu.VMEM((rows, width), F32)],
+            scratch_shapes=[block, pltpu.VMEM((rows, width), F32)] + [picks] * 4,
             compiler_params=PARAMS,
             name="far_mine" if mine else "far_theirs",
         )(codes, other_codes, sector_sizes, other_block, left_factors, right_factors, near)

time: 26.4 us -> 25.8 us (0.977)
  Pallas kernels: 8.05 us -> 6.66 us
  waiting for transfers between devices: 11.7 us -> 12.2 us
    pallas_call x2, Pallas kernels: 5.23 us -> 4.1 us  [far(): pl.pallas_call(functools.partial(far_kernel, mine), out_shape=jax.ShapeDt...]
    ppermute x1, starting transfers between devices: 0.07 us -> 0.34 us  [shards(): got = [lax.ppermute(theirs, 'group', hops[0])]]
  transfers between devices with their start and end apart: 5 -> 5, of which waited for: 2 -> 2; matrix products, arithmetic and copies ran while one was open for 0% -> 0% of each run, Pallas kernels for 17% -> 15%
where the time goes in v5:
time: 25.8 us; the launch traced here: 25.6 us
  waiting for transfers between devices  12.2 us (47%)
  Pallas kernels  6.66 us (26%)
  starting transfers between devices  6.01 us (23%)
  between operations  0.77 us (3%)
    ppermute x1, waiting for transfers between devices, shards(): other_codes = lax.ppermute(codes, 'sector', others)  8.11 us
    pallas_call x2, Pallas kernels, far(): pl.pallas_call(functools.partial(far_kernel, mine), out_shape=jax.ShapeDt...  4.1 us
    ppermute x1, waiting for transfers between devices, shards(): got = [lax.ppermute(theirs, 'group', hops[0])]  4.05 us
    ppermute x1, starting transfers between devices, shards(): other_codes = lax.ppermute(codes, 'sector', others)  2.11 us
    ppermute x1, starting transfers between devices, shards(): other_block = lax.ppermute(wavefunction, 'sector', others)  1.91 us
    ppermute x1, starting transfers between devices, shards(): friend_codes = lax.ppermute(codes, 'sector', friends)  1.65 us
    pallas_call x1, Pallas kernels, shards(): pl.pallas_call(codes_kernel, out_shape=jax.ShapeDtypeStruct(term_list.sha...  0.9 us
    pallas_call x1, Pallas kernels, shards(): pl.pallas_call(near_kernel, out_shape=jax.ShapeDtypeStruct((width, width)...  0.9 us
  transfers between devices with their start and end apart: 5, of which 2 were waited for; matrix products, arithmetic and copies ran while one was open for 0% of the time, Pallas kernels for 15%

profile of v5, /device:TPU:2, one launch (start us, length us, event | category | flops | bytes accessed | tf_op | source)
XLA Modules:
  0.0 25.6 jit_solution(16549993729693346266)
XLA Ops:
  0.0 0.0 collective-permute-start.3
  0.0 1.9 %collective-permute-start.1 = (bf16[1,512,512]{2,1,0:T(8,128)(2,1)}, bf16[1,512,512]{2,1,0:T(8,128)(2,1)S(1)}, u32[]{:S(2)}, u32[]{:S(2)}) collective-permute-start(bf16[1,512,512]{2,1,0:T(8,128)(2,1)} %own_block.1), channel_id=1, source_target_pairs={{1,2},{2,1},{3,4},{4,3},{5,6},{6,5},{7,8},{8,7},{9,10},{10,9},{11,... | collective-permute-start | bytes 1572872 | tf_op jit(solution)/shard_map/ppermute | solution.py:160
  2.6 0.0 copy-start
  2.6 0.0 copy-start.1
  2.6 0.0 copy-start.2
  2.6 0.0 copy-start.3
  2.6 0.9 %codes.1.own_codes = s32[4,3]{1,0:T(4,128)S(1)} custom-call(s32[4,3]{1,0:T(4,128)} %term_list.1, s32[1,1]{1,0:T(1,128)} %bitcast.1.term_counts), custom_call_target="tpu_custom_call" | custom-call | flops 4000000000 | bytes 16777216 | tf_op jit(solution)/shard_map/codes/pallas_call | solution.py:162
  3.5 1.7 %collective-permute-start.2 = (s32[4,3]{1,0:T(4,128)S(1)}, s32[4,3]{1,0:T(4,128)S(1)}, u32[]{:S(2)}, u32[]{:S(2)}) collective-permute-start(s32[4,3]{1,0:T(4,128)S(1)} %codes.1.own_codes), channel_id=1, source_target_pairs={{0,1},{1,0},{2,3},{3,2},{4,5},{5,4},{6,7},{7,6},{8,9},{9,8},{10,11... | collective-permute-start | bytes 152 | tf_op jit(solution)/shard_map/ppermute | solution.py:171
  5.2 2.1 %collective-permute-start = (s32[4,3]{1,0:T(4,128)S(1)}, s32[4,3]{1,0:T(4,128)S(1)}, u32[]{:S(2)}, u32[]{:S(2)}) collective-permute-start(s32[4,3]{1,0:T(4,128)S(1)} %codes.1.own_codes), channel_id=1, source_target_pairs={{1,2},{2,1},{3,4},{4,3},{5,6},{6,5},{7,8},{8,7},{9,10},{10,9},{11,... | collective-permute-start | bytes 152 | tf_op jit(solution)/shard_map/ppermute | solution.py:172
  7.3 0.0 collective-permute-done.2.friend_codes
  7.3 0.0 collective-permute-done.3.friend_block
  7.3 0.0 copy-done
  7.3 0.0 copy-done.1
  7.3 0.0 copy-done.2
  7.3 0.0 copy-done.3
  7.3 0.9 %near.1 = f32[512,512]{1,0:T(8,128)S(1)} custom-call(s32[4,3]{1,0:T(4,128)S(1)} %codes.1.own_codes, s32[4,3]{1,0:T(4,128)S(1)} %collective-permute-done.2.friend_codes, s32[16]{0:T(128)S(1)} %copy-done.3, bf16[1,512,512]{2,1,0:T(8,128)(2,1)S(1)} %copy-done.2, bf16[1,512,512]{2,1,0:T(8,128)(2,1)S(1)} %collective-permute-done.3.friend_block, ...), custom_call_target="tpu_custom_call" | custom-call | tf_op jit(solution)/shard_map/near/pallas_call | solution.py:173
  8.3 8.1 %collective-permute-done.other_codes = s32[4,3]{1,0:T(4,128)S(1)} collective-permute-done((s32[4,3]{1,0:T(4,128)S(1)}, s32[4,3]{1,0:T(4,128)S(1)}, u32[]{:S(2)}, u32[]{:S(2)}) %collective-permute-start) | collective-permute-done | bytes 80 | tf_op jit(solution)/shard_map/ppermute | solution.py:172
  16.4 0.0 collective-permute-done.1.other_block
  16.4 2.1 %far_theirs.1 = bf16[256,512]{1,0:T(8,128)(2,1)S(1)} custom-call(s32[4,3]{1,0:T(4,128)S(1)} %codes.1.own_codes, s32[4,3]{1,0:T(4,128)S(1)} %collective-permute-done.other_codes, s32[16]{0:T(128)S(1)} %copy-done.3, bf16[1,512,512]{2,1,0:T(8,128)(2,1)S(1)} %collective-permute-done.1.other_block, bf16[3,512,512]{2,1,0:T(8,128)(2,1)S(1)} %copy-done, ...), custom_call_target="tpu_custom_call" | custom-call | tf_op jit(solution)/shard_map/far_theirs/pallas_call | solution.py:186
  18.4 0.3 %collective-permute-start.4 = (bf16[256,512]{1,0:T(8,128)(2,1)S(1)}, bf16[256,512]{1,0:T(8,128)(2,1)S(1)}, u32[]{:S(2)}, u32[]{:S(2)}) collective-permute-start(bf16[256,512]{1,0:T(8,128)(2,1)S(1)} %far_theirs.1), channel_id=1, source_target_pairs={{0,16},{16,0},{1,17},{17,1},{2,18},{18,2},{3,19},{19,3},{4,20},{20... | collective-permute-start | bytes 786440 | tf_op jit(solution)/shard_map/ppermute | solution.py:199
  18.8 2.0 %far_mine.1.kept = f32[256,512]{1,0:T(8,128)S(1)} custom-call(s32[4,3]{1,0:T(4,128)S(1)} %codes.1.own_codes, s32[4,3]{1,0:T(4,128)S(1)} %collective-permute-done.other_codes, s32[16]{0:T(128)S(1)} %copy-done.3, bf16[1,512,512]{2,1,0:T(8,128)(2,1)S(1)} %collective-permute-done.1.other_block, bf16[3,512,512]{2,1,0:T(8,128)(2,1)S(1)} %copy-done, ...), custom_call_target="tpu_custom_call" | custom-call | tf_op jit(solution)/shard_map/far_mine/pallas_call | solution.py:186
  20.8 4.0 %collective-permute-done.4.refs_0_ = bf16[256,512]{1,0:T(8,128)(2,1)S(1)} collective-permute-done((bf16[256,512]{1,0:T(8,128)(2,1)S(1)}, bf16[256,512]{1,0:T(8,128)(2,1)S(1)}, u32[]{:S(2)}, u32[]{:S(2)}) %collective-permute-start.4) | collective-permute-done | bytes 262176 | tf_op jit(solution)/shard_map/ppermute | solution.py:199
  24.9 0.7 %last.1 = bf16[1,256,512]{2,1,0:T(8,128)(2,1)} custom-call(f32[256,512]{1,0:T(8,128)S(1)} %far_mine.1.kept, bf16[256,512]{1,0:T(8,128)(2,1)S(1)} %collective-permute-done.4.refs_0_), custom_call_target="tpu_custom_call" | custom-call | tf_op jit(solution)/shard_map/last/pallas_call | solution.py:209
Async XLA Ops:
  0.0 7.3 %collective-permute-start.3 = (bf16[1,512,512]{2,1,0:T(8,128)(2,1)}, bf16[1,512,512]{2,1,0:T(8,128)(2,1)S(1)}, u32[]{:S(2)}, u32[]{:S(2)}) collective-permute-start(bf16[1,512,512]{2,1,0:T(8,128)(2,1)} %own_block.1), channel_id=1, source_target_pairs={{0,1},{1,0},{2,3},{3,2},{4,5},{5,4},{6,7},{7,6},{8,9},{9,8},{10,11... | collective-permute-start | bytes 1572872 | tf_op jit(solution)/shard_map/ppermute | solution.py:161
  0.0 16.4 %collective-permute-start.1 = (bf16[1,512,512]{2,1,0:T(8,128)(2,1)}, bf16[1,512,512]{2,1,0:T(8,128)(2,1)S(1)}, u32[]{:S(2)}, u32[]{:S(2)}) collective-permute-start(bf16[1,512,512]{2,1,0:T(8,128)(2,1)} %own_block.1), channel_id=1, source_target_pairs={{1,2},{2,1},{3,4},{4,3},{5,6},{6,5},{7,8},{8,7},{9,10},{10,9},{11,... | collective-permute-start | bytes 1572872 | tf_op jit(solution)/shard_map/ppermute | solution.py:160
  2.6 4.7 %copy-start = (bf16[3,512,512]{2,1,0:T(8,128)(2,1)S(1)}, bf16[3,512,512]{2,1,0:T(8,128)(2,1)}, u32[]{:S(2)}) copy-start(bf16[3,512,512]{2,1,0:T(8,128)(2,1)} %left.5) | copy-start | bytes 4718596
  2.6 4.7 %copy-start.1 = (bf16[3,512,512]{2,1,0:T(8,128)(2,1)S(1)}, bf16[3,512,512]{2,1,0:T(8,128)(2,1)}, u32[]{:S(2)}) copy-start(bf16[3,512,512]{2,1,0:T(8,128)(2,1)} %right.5) | copy-start | bytes 4718596
  2.6 4.7 %copy-start.2 = (bf16[1,512,512]{2,1,0:T(8,128)(2,1)S(1)}, bf16[1,512,512]{2,1,0:T(8,128)(2,1)}, u32[]{:S(2)}) copy-start(bf16[1,512,512]{2,1,0:T(8,128)(2,1)} %own_block.1) | copy-start | bytes 1572868
  2.6 4.7 %copy-start.3 = (s32[16]{0:T(128)S(1)}, s32[16]{0:T(128)}, u32[]{:S(2)}) copy-start(s32[16]{0:T(128)} %sizes.5) | copy-start | bytes 196
  3.5 3.8 %collective-permute-start.2 = (s32[4,3]{1,0:T(4,128)S(1)}, s32[4,3]{1,0:T(4,128)S(1)}, u32[]{:S(2)}, u32[]{:S(2)}) collective-permute-start(s32[4,3]{1,0:T(4,128)S(1)} %codes.1.own_codes), channel_id=1, source_target_pairs={{0,1},{1,0},{2,3},{3,2},{4,5},{5,4},{6,7},{7,6},{8,9},{9,8},{10,11... | collective-permute-start | bytes 152 | tf_op jit(solution)/shard_map/ppermute | solution.py:171
  5.2 11.2 %collective-permute-start = (s32[4,3]{1,0:T(4,128)S(1)}, s32[4,3]{1,0:T(4,128)S(1)}, u32[]{:S(2)}, u32[]{:S(2)}) collective-permute-start(s32[4,3]{1,0:T(4,128)S(1)} %codes.1.own_codes), channel_id=1, source_target_pairs={{1,2},{2,1},{3,4},{4,3},{5,6},{6,5},{7,8},{8,7},{9,10},{10,9},{11,... | collective-permute-start | bytes 152 | tf_op jit(solution)/shard_map/ppermute | solution.py:172
  18.4 6.4 %collective-permute-start.4 = (bf16[256,512]{1,0:T(8,128)(2,1)S(1)}, bf16[256,512]{1,0:T(8,128)(2,1)S(1)}, u32[]{:S(2)}, u32[]{:S(2)}) collective-permute-start(bf16[256,512]{1,0:T(8,128)(2,1)S(1)} %far_theirs.1), channel_id=1, source_target_pairs={{0,16},{16,0},{1,17},{17,1},{2,18},{18,2},{3,19},{19,3},{4,20},{20... | collective-permute-start | bytes 786440 | tf_op jit(solution)/shard_map/ppermute | solution.py:199

commit v6 on v2

--- a/solution.py
+++ b/solution.py
@@ -42,6 +42,12 @@
     return jnp.where((rows < size) & (cols < size), block, jnp.zeros_like(block))
 
 
+def cleaned(block, size):
+    rows = lax.broadcasted_iota(jnp.int32, (block.shape[0], 1), 0) < size
+    cols = lax.broadcasted_iota(jnp.int32, (1, block.shape[1]), 1) < size
+    return block * rows.astype(BF16) * cols.astype(BF16)
+
+
 def live_terms(codes, owner, want, action):
     for k in range(codes.shape[0]):
         @pl.when(owner + codes[k, 0] - 2 == want)
@@ -54,11 +60,17 @@
     codes[...] = jnp.where(slot < term_counts[...], term_list[...] + 1, 0)
 
 
-def near_kernel(own_codes, friend_codes, sizes, own_block, friend_block, left, right, acc, clean, friend_clean):
+def near_kernel(own_codes, friend_codes, sizes, own_block, friend_block, left, right,
+                acc, plan, clean, friend_clean, lefts, rights):
     here = lax.axis_index("sector")
     friend = friend_of(here)
-    clean[...] = masked(own_block[0], sizes[here])
-    friend_clean[...] = masked(friend_block[0], sizes[jnp.minimum(friend, sizes.shape[0] - 1)])
+    other = other_of(here)
+    slots = own_codes.shape[0]
+    adjoints = picked(own_codes, here, other, lefts, rights)
+    scalars = [sizes[here], sizes[jnp.clip(other, 0, sizes.shape[0] - 1)], adjoints]
+    plan[...] = written(scalars + [lefts[k] for k in range(slots)] + [rights[k] for k in range(slots)])
+    clean[...] = cleaned(own_block[0], sizes[here])
+    friend_clean[...] = cleaned(friend_block[0], sizes[jnp.minimum(friend, sizes.shape[0] - 1)])
     acc[...] = jnp.zeros_like(acc)
 
     def self_term(l, r):
@@ -70,20 +82,89 @@
     live_terms(friend_codes, friend, here, lambda l, r: forward(acc, left.at[l], friend_clean, right.at[r]))
 
 
-def far_kernel(mine, own_codes, other_codes, sizes, other_block, left, right, near, out, clean, acc):
+def picked(codes, owner, want, lefts, rights):
+    live = jnp.int32(0)
+    for k in range(codes.shape[0]):
+        lefts[k] = 0
+        rights[k] = 0
+    for k in range(codes.shape[0]):
+        lefts[live] = codes[k, 1] - 1
+        rights[live] = codes[k, 2] - 1
+        live += (owner + codes[k, 0] - 2 == want).astype(jnp.int32)
+    return live
+
+
+def written(values):
+    lane = lax.broadcasted_iota(jnp.int32, (1, len(values)), 1)
+    row = jnp.zeros((1, len(values)), jnp.int32)
+    for i, value in enumerate(values):
+        row = jnp.where(lane == i, value, row)
+    return row
+
+
+def far_kernel(mine, plan, other_codes, other_block, left, right, near, out, clean, acc, lefts, rights):
     here = lax.axis_index("sector")
     other = other_of(here)
     share = out.shape[0]
-    clean[...] = masked(other_block[0], sizes[jnp.clip(other, 0, sizes.shape[0] - 1)])
+    slots = other_codes.shape[0]
+    size, adjoints = plan[0, 0], plan[0, 2]
+    clean[...] = cleaned(other_block[0], plan[0, 1])
+    forwards = picked(other_codes, other, here, lefts, rights)
 
     def run(rows):
         first = rows.start or 0
         acc[...] = near[rows, :]
-        live_terms(own_codes, here, other,
-                   lambda l, r: adjoint(acc, left.at[l, :, rows], clean, right.at[r]))
-        live_terms(other_codes, other, here,
-                   lambda l, r: forward(acc, left.at[l, rows, :], clean, right.at[r]))
-        out[...] = masked(acc[...], sizes[here], first).astype(out.dtype)
+
+        def forward_left(i):
+            return left[lefts[i], rows, :]
+
+        def adjoint_left(i):
+            return left[plan[0, 3 + i], :, rows]
+
+        def adjoint_right(i):
+            return right[plan[0, 3 + slots + i]]
+
+        def forward_pair(i, carry):
+            a = jnp.concatenate([forward_left(2 * i), forward_left(2 * i + 1)], axis=0)
+            b = jnp.concatenate([right[rights[2 * i]], right[rights[2 * i + 1]]], axis=0)
+            middle = dot(a, clean[...], 1, 0).astype(BF16)
+            acc[...] += dot(jnp.concatenate([middle[:share], middle[share:]], axis=1), b, 1, 0)
+            return carry
+
+        def adjoint_pair(i, carry):
+            a = jnp.concatenate([adjoint_left(2 * i), adjoint_left(2 * i + 1)], axis=1)
+            b = jnp.concatenate([adjoint_right(2 * i), adjoint_right(2 * i + 1)], axis=1)
+            middle = dot(a, clean[...], 0, 0).astype(BF16)
+            acc[...] += dot(jnp.concatenate([middle[:share], middle[share:]], axis=1), b, 1, 1)
+            return carry
+
+        def forward_one():
+            middle = dot(forward_left(forwards - 1), clean[...], 1, 0).astype(BF16)
+            return dot(middle, right[rights[forwards - 1]], 1, 0)
+
+        def adjoint_one():
+            middle = dot(adjoint_left(adjoints - 1), clean[...], 0, 0).astype(BF16)
+            return dot(middle, adjoint_right(adjoints - 1), 1, 1)
+
+        @pl.when(first < size)
+        def _():
+            lax.fori_loop(0, forwards // 2, forward_pair, 0)
+            lax.fori_loop(0, adjoints // 2, adjoint_pair, 0)
+            rest_forward, rest_adjoint = forwards % 2 == 1, adjoints % 2 == 1
+
+            @pl.when(rest_forward & rest_adjoint)
+            def _():
+                acc[...] += forward_one() + adjoint_one()
+
+            @pl.when(rest_forward & ~rest_adjoint)
+            def _():
+                acc[...] += forward_one()
+
+            @pl.when(rest_adjoint & ~rest_forward)
+            def _():
+                acc[...] += adjoint_one()
+
+        out[...] = masked(acc[...], size, first).astype(out.dtype)
 
     if share == near.shape[0]:
         run(slice(None))
@@ -119,17 +200,22 @@
         in_specs=[VMEM, VMEM],
         out_specs=VMEM,
         compiler_params=pltpu.CompilerParams(vmem_limit_bytes=2**20),
-        cost_estimate=pl.CostEstimate(flops=10**9, transcendentals=0, bytes_accessed=4 * 2**20),
+        cost_estimate=pl.CostEstimate(flops=4 * 10**9, transcendentals=0, bytes_accessed=2**24),
         name="codes",
     )(hbm(term_list), term_counts[:, None])
     friend_codes = lax.ppermute(codes, "sector", friends)
     other_codes = lax.ppermute(codes, "sector", others)
-    near = pl.pallas_call(
+    slots = term_list.shape[0]
+    picks = pltpu.SMEM((slots,), jnp.int32)
+    near, plan = pl.pallas_call(
         near_kernel,
-        out_shape=jax.ShapeDtypeStruct((width, width), F32),
+        out_shape=[
+            jax.ShapeDtypeStruct((width, width), F32),
+            jax.ShapeDtypeStruct((1, 3 + 2 * slots), jnp.int32),
+        ],
         in_specs=[SMEM, SMEM, SMEM, VMEM, VMEM, VMEM, VMEM],
-        out_specs=VMEM,
-        scratch_shapes=[block, block],
+        out_specs=[VMEM, VMEM],
+        scratch_shapes=[block, block, picks, picks],
         compiler_params=PARAMS,
         name="near",
     )(codes, friend_codes, sector_sizes, wavefunction, friend_block, left_factors, right_factors)
@@ -138,12 +224,12 @@
         return pl.pallas_call(
             functools.partial(far_kernel, mine),
             out_shape=jax.ShapeDtypeStruct((rows, width), dtype),
-            in_specs=[SMEM, SMEM, SMEM, VMEM, VMEM, VMEM, VMEM],
+            in_specs=[SMEM, SMEM, VMEM, VMEM, VMEM, VMEM],
             out_specs=VMEM,
-            scratch_shapes=[block, pltpu.VMEM((rows, width), F32)],
+            scratch_shapes=[block, pltpu.VMEM((rows, width), F32), picks, picks],
             compiler_params=PARAMS,
             name="far_mine" if mine else "far_theirs",
-        )(codes, other_codes, sector_sizes, other_block, left_factors, right_factors, near)
+        )(plan, other_codes, other_block, left_factors, right_factors, near)
 
     hops = [[(g, (g + hop) % groups) for g in range(groups)] for hop in range(1, groups)]
     if groups == 2 and share % 128 == 0:

time: 26.4 us -> 26.5 us (level)
  the two profiles are of different devices: /device:TPU:2 before, /device:TPU:22 now
where the time goes in v6:
time: 26.5 us; the launch traced here: 26.4 us
  waiting for transfers between devices  11.1 us (42%)
  starting transfers between devices  8.51 us (32%)
  Pallas kernels  6.05 us (23%)
  between operations  0.73 us (3%)
    ppermute x1, waiting for transfers between devices, shards(): got = [lax.ppermute(theirs, 'group', hops[0])]  6.33 us
    ppermute x1, waiting for transfers between devices, shards(): other_codes = lax.ppermute(codes, 'sector', others)  3.9 us
    ppermute x1, starting transfers between devices, shards(): other_codes = lax.ppermute(codes, 'sector', others)  3.13 us
    pallas_call x1, Pallas kernels, shards(): pl.pallas_call(near_kernel, out_shape=[jax.ShapeDtypeStruct((width, width...  2.85 us
    ppermute x1, starting transfers between devices, shards(): other_block = lax.ppermute(wavefunction, 'sector', others)  2.54 us
    pallas_call x2, Pallas kernels, far(): pl.pallas_call(functools.partial(far_kernel, mine), out_shape=jax.ShapeDt...  1.54 us
    ppermute x1, starting transfers between devices, shards(): friend_codes = lax.ppermute(codes, 'sector', friends)  1.47 us
    ppermute x1, starting transfers between devices, shards(): got = [lax.ppermute(theirs, 'group', hops[0])]  1.37 us
  transfers between devices with their start and end apart: 5, of which 3 were waited for; matrix products, arithmetic and copies ran while one was open for 0% of the time, Pallas kernels for 17%

profile of v6, /device:TPU:22, one launch (start us, length us, event | category | flops | bytes accessed | tf_op | source)
XLA Modules:
  0.0 26.4 jit_solution(10318003526564552744)
XLA Ops:
  0.0 0.0 collective-permute-start.1
  0.0 2.5 %collective-permute-start.3 = (bf16[1,512,512]{2,1,0:T(8,128)(2,1)}, bf16[1,512,512]{2,1,0:T(8,128)(2,1)S(1)}, u32[]{:S(2)}, u32[]{:S(2)}) collective-permute-start(bf16[1,512,512]{2,1,0:T(8,128)(2,1)} %own_block.1), channel_id=1, source_target_pairs={{1,2},{2,1},{3,4},{4,3},{5,6},{6,5},{7,8},{8,7},{9,10},{10,9},{11,... | collective-permute-start | bytes 1572872 | tf_op jit(solution)/shard_map/ppermute | solution.py:195
  3.2 0.0 copy-start
  3.2 0.0 copy-start.1
  3.2 0.0 copy-start.2
  3.2 0.0 copy-start.3
  3.2 0.9 %codes.1.own_codes = s32[4,3]{1,0:T(4,128)S(1)} custom-call(s32[4,3]{1,0:T(4,128)} %term_list.1, s32[1,1]{1,0:T(1,128)} %bitcast.1.term_counts), custom_call_target="tpu_custom_call" | custom-call | flops 4000000000 | bytes 16777216 | tf_op jit(solution)/shard_map/codes/pallas_call | solution.py:197
  4.1 3.1 %collective-permute-start.2 = (s32[4,3]{1,0:T(4,128)S(1)}, s32[4,3]{1,0:T(4,128)S(1)}, u32[]{:S(2)}, u32[]{:S(2)}) collective-permute-start(s32[4,3]{1,0:T(4,128)S(1)} %codes.1.own_codes), channel_id=1, source_target_pairs={{1,2},{2,1},{3,4},{4,3},{5,6},{6,5},{7,8},{8,7},{9,10},{10,9},{11,... | collective-permute-start | bytes 152 | tf_op jit(solution)/shard_map/ppermute | solution.py:207
  7.3 1.5 %collective-permute-start = (s32[4,3]{1,0:T(4,128)S(1)}, s32[4,3]{1,0:T(4,128)S(1)}, u32[]{:S(2)}, u32[]{:S(2)}) collective-permute-start(s32[4,3]{1,0:T(4,128)S(1)} %codes.1.own_codes), channel_id=1, source_target_pairs={{0,1},{1,0},{2,3},{3,2},{4,5},{5,4},{6,7},{7,6},{8,9},{9,8},{10,11... | collective-permute-start | bytes 152 | tf_op jit(solution)/shard_map/ppermute | solution.py:206
  8.8 0.8 %collective-permute-done.friend_codes = s32[4,3]{1,0:T(4,128)S(1)} collective-permute-done((s32[4,3]{1,0:T(4,128)S(1)}, s32[4,3]{1,0:T(4,128)S(1)}, u32[]{:S(2)}, u32[]{:S(2)}) %collective-permute-start) | collective-permute-done | bytes 80 | tf_op jit(solution)/shard_map/ppermute | solution.py:206
  9.6 0.0 collective-permute-done.1.friend_block
  9.6 0.0 copy-done
  9.6 0.0 copy-done.1
  9.6 0.0 copy-done.2
  9.6 0.0 copy-done.3
  9.6 2.9 %near.1 = (f32[512,512]{1,0:T(8,128)S(1)}, s32[1,11]{1,0:T(1,128)S(1)}) custom-call(s32[4,3]{1,0:T(4,128)S(1)} %codes.1.own_codes, s32[4,3]{1,0:T(4,128)S(1)} %collective-permute-done.friend_codes, s32[16]{0:T(128)S(1)} %copy-done.3, bf16[1,512,512]{2,1,0:T(8,128)(2,1)S(1)} %copy-done.2, bf16[1,512,512]{2,1,0:T(8,128)(2,1)S(1)} %collective-permute-done.1.friend_block, ...), custom_call_target="tpu_custom_call" | custom-call | tf_op jit(solution)/shard_map/near/pallas_call | solution.py:210
  12.5 3.9 %collective-permute-done.2.other_codes = s32[4,3]{1,0:T(4,128)S(1)} collective-permute-done((s32[4,3]{1,0:T(4,128)S(1)}, s32[4,3]{1,0:T(4,128)S(1)}, u32[]{:S(2)}, u32[]{:S(2)}) %collective-permute-start.2) | collective-permute-done | bytes 80 | tf_op jit(solution)/shard_map/ppermute | solution.py:207
  16.4 0.0 collective-permute-done.3.other_block
  16.4 0.8 %far_theirs.1 = bf16[256,512]{1,0:T(8,128)(2,1)S(1)} custom-call(s32[1,11]{1,0:T(1,128)S(1)} %get-tuple-element.7.plan, s32[4,3]{1,0:T(4,128)S(1)} %collective-permute-done.2.other_codes, bf16[1,512,512]{2,1,0:T(8,128)(2,1)S(1)} %collective-permute-done.3.other_block, bf16[3,512,512]{2,1,0:T(8,128)(2,1)S(1)} %copy-done, bf16[3,512,512]{2,1,0:T(8,128)(2,1)S(1)} %copy-done.1, ...), custom_call_target="tpu_custom_call" | custom-call | tf_op jit(solution)/shard_map/far_theirs/pallas_call | solution.py:224
  17.1 1.4 %collective-permute-start.4 = (bf16[256,512]{1,0:T(8,128)(2,1)S(1)}, bf16[256,512]{1,0:T(8,128)(2,1)S(1)}, u32[]{:S(2)}, u32[]{:S(2)}) collective-permute-start(bf16[256,512]{1,0:T(8,128)(2,1)S(1)} %far_theirs.1), channel_id=1, source_target_pairs={{0,16},{16,0},{1,17},{17,1},{2,18},{18,2},{3,19},{19,3},{4,20},{20... | collective-permute-start | bytes 786440 | tf_op jit(solution)/shard_map/ppermute | solution.py:237
  18.5 0.8 %far_mine.1.kept = f32[256,512]{1,0:T(8,128)S(1)} custom-call(s32[1,11]{1,0:T(1,128)S(1)} %get-tuple-element.7.plan, s32[4,3]{1,0:T(4,128)S(1)} %collective-permute-done.2.other_codes, bf16[1,512,512]{2,1,0:T(8,128)(2,1)S(1)} %collective-permute-done.3.other_block, bf16[3,512,512]{2,1,0:T(8,128)(2,1)S(1)} %copy-done, bf16[3,512,512]{2,1,0:T(8,128)(2,1)S(1)} %copy-done.1, ...), custom_call_target="tpu_custom_call" | custom-call | tf_op jit(solution)/shard_map/far_mine/pallas_call | solution.py:224
  19.3 6.3 %collective-permute-done.4.refs_0_ = bf16[256,512]{1,0:T(8,128)(2,1)S(1)} collective-permute-done((bf16[256,512]{1,0:T(8,128)(2,1)S(1)}, bf16[256,512]{1,0:T(8,128)(2,1)S(1)}, u32[]{:S(2)}, u32[]{:S(2)}) %collective-permute-start.4) | collective-permute-done | bytes 262176 | tf_op jit(solution)/shard_map/ppermute | solution.py:237
  25.6 0.7 %last.1 = bf16[1,256,512]{2,1,0:T(8,128)(2,1)} custom-call(f32[256,512]{1,0:T(8,128)S(1)} %far_mine.1.kept, bf16[256,512]{1,0:T(8,128)(2,1)S(1)} %collective-permute-done.4.refs_0_), custom_call_target="tpu_custom_call" | custom-call | tf_op jit(solution)/shard_map/last/pallas_call | solution.py:247
Async XLA Ops:
  0.0 9.6 %collective-permute-start.1 = (bf16[1,512,512]{2,1,0:T(8,128)(2,1)}, bf16[1,512,512]{2,1,0:T(8,128)(2,1)S(1)}, u32[]{:S(2)}, u32[]{:S(2)}) collective-permute-start(bf16[1,512,512]{2,1,0:T(8,128)(2,1)} %own_block.1), channel_id=1, source_target_pairs={{0,1},{1,0},{2,3},{3,2},{4,5},{5,4},{6,7},{7,6},{8,9},{9,8},{10,11... | collective-permute-start | bytes 1572872 | tf_op jit(solution)/shard_map/ppermute | solution.py:196
  0.0 16.4 %collective-permute-start.3 = (bf16[1,512,512]{2,1,0:T(8,128)(2,1)}, bf16[1,512,512]{2,1,0:T(8,128)(2,1)S(1)}, u32[]{:S(2)}, u32[]{:S(2)}) collective-permute-start(bf16[1,512,512]{2,1,0:T(8,128)(2,1)} %own_block.1), channel_id=1, source_target_pairs={{1,2},{2,1},{3,4},{4,3},{5,6},{6,5},{7,8},{8,7},{9,10},{10,9},{11,... | collective-permute-start | bytes 1572872 | tf_op jit(solution)/shard_map/ppermute | solution.py:195
  3.2 6.4 %copy-start = (bf16[3,512,512]{2,1,0:T(8,128)(2,1)S(1)}, bf16[3,512,512]{2,1,0:T(8,128)(2,1)}, u32[]{:S(2)}) copy-start(bf16[3,512,512]{2,1,0:T(8,128)(2,1)} %left.5) | copy-start | bytes 4718596
  3.2 6.4 %copy-start.1 = (bf16[3,512,512]{2,1,0:T(8,128)(2,1)S(1)}, bf16[3,512,512]{2,1,0:T(8,128)(2,1)}, u32[]{:S(2)}) copy-start(bf16[3,512,512]{2,1,0:T(8,128)(2,1)} %right.5) | copy-start | bytes 4718596
  3.2 6.4 %copy-start.2 = (bf16[1,512,512]{2,1,0:T(8,128)(2,1)S(1)}, bf16[1,512,512]{2,1,0:T(8,128)(2,1)}, u32[]{:S(2)}) copy-start(bf16[1,512,512]{2,1,0:T(8,128)(2,1)} %own_block.1) | copy-start | bytes 1572868
  3.2 6.4 %copy-start.3 = (s32[16]{0:T(128)S(1)}, s32[16]{0:T(128)}, u32[]{:S(2)}) copy-start(s32[16]{0:T(128)} %sizes.1) | copy-start | bytes 196
  4.1 12.2 %collective-permute-start.2 = (s32[4,3]{1,0:T(4,128)S(1)}, s32[4,3]{1,0:T(4,128)S(1)}, u32[]{:S(2)}, u32[]{:S(2)}) collective-permute-start(s32[4,3]{1,0:T(4,128)S(1)} %codes.1.own_codes), channel_id=1, source_target_pairs={{1,2},{2,1},{3,4},{4,3},{5,6},{6,5},{7,8},{8,7},{9,10},{10,9},{11,... | collective-permute-start | bytes 152 | tf_op jit(solution)/shard_map/ppermute | solution.py:207
  7.3 2.3 %collective-permute-start = (s32[4,3]{1,0:T(4,128)S(1)}, s32[4,3]{1,0:T(4,128)S(1)}, u32[]{:S(2)}, u32[]{:S(2)}) collective-permute-start(s32[4,3]{1,0:T(4,128)S(1)} %codes.1.own_codes), channel_id=1, source_target_pairs={{0,1},{1,0},{2,3},{3,2},{4,5},{5,4},{6,7},{7,6},{8,9},{9,8},{10,11... | collective-permute-start | bytes 152 | tf_op jit(solution)/shard_map/ppermute | solution.py:206
  17.1 8.5 %collective-permute-start.4 = (bf16[256,512]{1,0:T(8,128)(2,1)S(1)}, bf16[256,512]{1,0:T(8,128)(2,1)S(1)}, u32[]{:S(2)}, u32[]{:S(2)}) collective-permute-start(bf16[256,512]{1,0:T(8,128)(2,1)S(1)} %far_theirs.1), channel_id=1, source_target_pairs={{0,16},{16,0},{1,17},{17,1},{2,18},{18,2},{3,19},{19,3},{4,20},{20... | collective-permute-start | bytes 786440 | tf_op jit(solution)/shard_map/ppermute | solution.py:237

commit v7 on v6

--- a/solution.py
+++ b/solution.py
@@ -176,10 +176,20 @@
 
 
 def last_kernel(kept, *refs):
-    total = kept[...]
-    for part in refs[:-1]:
-        total = total + part[...].astype(F32)
-    refs[-1][0] = total.astype(BF16)
+    parts, (out, ready, sems) = refs[:-3], refs[-3:]
+    pieces = sems.shape[0]
+    rows = kept.shape[0] // pieces
+    copies = []
+    for i in range(pieces):
+        piece = slice(i * rows, (i + 1) * rows)
+        total = kept[piece, :]
+        for part in parts:
+            total = total + part[piece, :].astype(F32)
+        ready[piece, :] = total.astype(BF16)
+        copies.append(pltpu.make_async_copy(ready.at[piece, :], out.at[0, piece, :], sems.at[i]))
+        copies[-1].start()
+    for copy in copies:
+        copy.wait()
 
 
 def shards(wavefunction, left_factors, right_factors, term_list, term_counts, sector_sizes):
@@ -248,7 +258,8 @@
         last_kernel,
         out_shape=jax.ShapeDtypeStruct((1, share, width), BF16),
         in_specs=[VMEM] * (1 + len(got)),
-        out_specs=VMEM,
+        out_specs=pl.BlockSpec(memory_space=pltpu.HBM),
+        scratch_shapes=[pltpu.VMEM((share, width), BF16), pltpu.SemaphoreType.DMA((2,))],
         compiler_params=PARAMS,
         name="last",
     )(kept, *got)

time: 26.5 us -> 26.5 us (level)
  no operation moved by 1% of the time
where the time goes in v7:
time: 26.5 us; the launch traced here: 26.4 us
  waiting for transfers between devices  11.1 us (42%)
  starting transfers between devices  8.51 us (32%)
  Pallas kernels  6.04 us (23%)
  between operations  0.73 us (3%)
    ppermute x1, waiting for transfers between devices, shards(): got = [lax.ppermute(theirs, 'group', hops[0])]  6.33 us
    ppermute x1, waiting for transfers between devices, shards(): other_codes = lax.ppermute(codes, 'sector', others)  3.9 us
    ppermute x1, starting transfers between devices, shards(): other_codes = lax.ppermute(codes, 'sector', others)  3.13 us
    pallas_call x1, Pallas kernels, shards(): pl.pallas_call(near_kernel, out_shape=[jax.ShapeDtypeStruct((width, width...  2.85 us
    ppermute x1, starting transfers between devices, shards(): other_block = lax.ppermute(wavefunction, 'sector', others)  2.54 us
    pallas_call x2, Pallas kernels, far(): pl.pallas_call(functools.partial(far_kernel, mine), out_shape=jax.ShapeDt...  1.54 us
    ppermute x1, starting transfers between devices, shards(): friend_codes = lax.ppermute(codes, 'sector', friends)  1.47 us
    ppermute x1, starting transfers between devices, shards(): got = [lax.ppermute(theirs, 'group', hops[0])]  1.37 us
  transfers between devices with their start and end apart: 5, of which 3 were waited for; matrix products, arithmetic and copies ran while one was open for 0% of the time, Pallas kernels for 17%

profile of v7, /device:TPU:22, one launch (start us, length us, event | category | flops | bytes accessed | tf_op | source)
XLA Modules:
  0.0 26.4 jit_solution(15516371709088379941)
XLA Ops:
  0.0 0.0 collective-permute-start.1
  0.0 2.5 %collective-permute-start.3 = (bf16[1,512,512]{2,1,0:T(8,128)(2,1)}, bf16[1,512,512]{2,1,0:T(8,128)(2,1)S(1)}, u32[]{:S(2)}, u32[]{:S(2)}) collective-permute-start(bf16[1,512,512]{2,1,0:T(8,128)(2,1)} %own_block.1), channel_id=1, source_target_pairs={{1,2},{2,1},{3,4},{4,3},{5,6},{6,5},{7,8},{8,7},{9,10},{10,9},{11,... | collective-permute-start | bytes 1572872 | tf_op jit(solution)/shard_map/ppermute | solution.py:205
  3.2 0.0 copy-start
  3.2 0.0 copy-start.1
  3.2 0.0 copy-start.2
  3.2 0.0 copy-start.3
  3.2 0.9 %codes.1.own_codes = s32[4,3]{1,0:T(4,128)S(1)} custom-call(s32[4,3]{1,0:T(4,128)} %term_list.1, s32[1,1]{1,0:T(1,128)} %bitcast.1.term_counts), custom_call_target="tpu_custom_call" | custom-call | flops 4000000000 | bytes 16777216 | tf_op jit(solution)/shard_map/codes/pallas_call | solution.py:207
  4.1 3.1 %collective-permute-start.2 = (s32[4,3]{1,0:T(4,128)S(1)}, s32[4,3]{1,0:T(4,128)S(1)}, u32[]{:S(2)}, u32[]{:S(2)}) collective-permute-start(s32[4,3]{1,0:T(4,128)S(1)} %codes.1.own_codes), channel_id=1, source_target_pairs={{1,2},{2,1},{3,4},{4,3},{5,6},{6,5},{7,8},{8,7},{9,10},{10,9},{11,... | collective-permute-start | bytes 152 | tf_op jit(solution)/shard_map/ppermute | solution.py:217
  7.3 1.5 %collective-permute-start = (s32[4,3]{1,0:T(4,128)S(1)}, s32[4,3]{1,0:T(4,128)S(1)}, u32[]{:S(2)}, u32[]{:S(2)}) collective-permute-start(s32[4,3]{1,0:T(4,128)S(1)} %codes.1.own_codes), channel_id=1, source_target_pairs={{0,1},{1,0},{2,3},{3,2},{4,5},{5,4},{6,7},{7,6},{8,9},{9,8},{10,11... | collective-permute-start | bytes 152 | tf_op jit(solution)/shard_map/ppermute | solution.py:216
  8.8 0.8 %collective-permute-done.friend_codes = s32[4,3]{1,0:T(4,128)S(1)} collective-permute-done((s32[4,3]{1,0:T(4,128)S(1)}, s32[4,3]{1,0:T(4,128)S(1)}, u32[]{:S(2)}, u32[]{:S(2)}) %collective-permute-start) | collective-permute-done | bytes 80 | tf_op jit(solution)/shard_map/ppermute | solution.py:216
  9.6 0.0 collective-permute-done.1.friend_block
  9.6 0.0 copy-done
  9.6 0.0 copy-done.1
  9.6 0.0 copy-done.2
  9.6 0.0 copy-done.3
  9.6 2.9 %near.1 = (f32[512,512]{1,0:T(8,128)S(1)}, s32[1,11]{1,0:T(1,128)S(1)}) custom-call(s32[4,3]{1,0:T(4,128)S(1)} %codes.1.own_codes, s32[4,3]{1,0:T(4,128)S(1)} %collective-permute-done.friend_codes, s32[16]{0:T(128)S(1)} %copy-done.3, bf16[1,512,512]{2,1,0:T(8,128)(2,1)S(1)} %copy-done.2, bf16[1,512,512]{2,1,0:T(8,128)(2,1)S(1)} %collective-permute-done.1.friend_block, ...), custom_call_target="tpu_custom_call" | custom-call | tf_op jit(solution)/shard_map/near/pallas_call | solution.py:220
  12.5 3.9 %collective-permute-done.2.other_codes = s32[4,3]{1,0:T(4,128)S(1)} collective-permute-done((s32[4,3]{1,0:T(4,128)S(1)}, s32[4,3]{1,0:T(4,128)S(1)}, u32[]{:S(2)}, u32[]{:S(2)}) %collective-permute-start.2) | collective-permute-done | bytes 80 | tf_op jit(solution)/shard_map/ppermute | solution.py:217
  16.4 0.0 collective-permute-done.3.other_block
  16.4 0.8 %far_theirs.1 = bf16[256,512]{1,0:T(8,128)(2,1)S(1)} custom-call(s32[1,11]{1,0:T(1,128)S(1)} %get-tuple-element.7.plan, s32[4,3]{1,0:T(4,128)S(1)} %collective-permute-done.2.other_codes, bf16[1,512,512]{2,1,0:T(8,128)(2,1)S(1)} %collective-permute-done.3.other_block, bf16[3,512,512]{2,1,0:T(8,128)(2,1)S(1)} %copy-done, bf16[3,512,512]{2,1,0:T(8,128)(2,1)S(1)} %copy-done.1, ...), custom_call_target="tpu_custom_call" | custom-call | tf_op jit(solution)/shard_map/far_theirs/pallas_call | solution.py:234
  17.1 1.4 %collective-permute-start.4 = (bf16[256,512]{1,0:T(8,128)(2,1)S(1)}, bf16[256,512]{1,0:T(8,128)(2,1)S(1)}, u32[]{:S(2)}, u32[]{:S(2)}) collective-permute-start(bf16[256,512]{1,0:T(8,128)(2,1)S(1)} %far_theirs.1), channel_id=1, source_target_pairs={{0,16},{16,0},{1,17},{17,1},{2,18},{18,2},{3,19},{19,3},{4,20},{20... | collective-permute-start | bytes 786440 | tf_op jit(solution)/shard_map/ppermute | solution.py:247
  18.5 0.8 %far_mine.1.kept = f32[256,512]{1,0:T(8,128)S(1)} custom-call(s32[1,11]{1,0:T(1,128)S(1)} %get-tuple-element.7.plan, s32[4,3]{1,0:T(4,128)S(1)} %collective-permute-done.2.other_codes, bf16[1,512,512]{2,1,0:T(8,128)(2,1)S(1)} %collective-permute-done.3.other_block, bf16[3,512,512]{2,1,0:T(8,128)(2,1)S(1)} %copy-done, bf16[3,512,512]{2,1,0:T(8,128)(2,1)S(1)} %copy-done.1, ...), custom_call_target="tpu_custom_call" | custom-call | tf_op jit(solution)/shard_map/far_mine/pallas_call | solution.py:234
  19.3 6.3 %collective-permute-done.4.refs_0_ = bf16[256,512]{1,0:T(8,128)(2,1)S(1)} collective-permute-done((bf16[256,512]{1,0:T(8,128)(2,1)S(1)}, bf16[256,512]{1,0:T(8,128)(2,1)S(1)}, u32[]{:S(2)}, u32[]{:S(2)}) %collective-permute-start.4) | collective-permute-done | bytes 262176 | tf_op jit(solution)/shard_map/ppermute | solution.py:247
  25.6 0.7 %last.1 = bf16[1,256,512]{2,1,0:T(8,128)(2,1)} custom-call(f32[256,512]{1,0:T(8,128)S(1)} %far_mine.1.kept, bf16[256,512]{1,0:T(8,128)(2,1)S(1)} %collective-permute-done.4.refs_0_), custom_call_target="tpu_custom_call" | custom-call | tf_op jit(solution)/shard_map/last/pallas_call | solution.py:257
Async XLA Ops:
  0.0 9.6 %collective-permute-start.1 = (bf16[1,512,512]{2,1,0:T(8,128)(2,1)}, bf16[1,512,512]{2,1,0:T(8,128)(2,1)S(1)}, u32[]{:S(2)}, u32[]{:S(2)}) collective-permute-start(bf16[1,512,512]{2,1,0:T(8,128)(2,1)} %own_block.1), channel_id=1, source_target_pairs={{0,1},{1,0},{2,3},{3,2},{4,5},{5,4},{6,7},{7,6},{8,9},{9,8},{10,11... | collective-permute-start | bytes 1572872 | tf_op jit(solution)/shard_map/ppermute | solution.py:206
  0.0 16.4 %collective-permute-start.3 = (bf16[1,512,512]{2,1,0:T(8,128)(2,1)}, bf16[1,512,512]{2,1,0:T(8,128)(2,1)S(1)}, u32[]{:S(2)}, u32[]{:S(2)}) collective-permute-start(bf16[1,512,512]{2,1,0:T(8,128)(2,1)} %own_block.1), channel_id=1, source_target_pairs={{1,2},{2,1},{3,4},{4,3},{5,6},{6,5},{7,8},{8,7},{9,10},{10,9},{11,... | collective-permute-start | bytes 1572872 | tf_op jit(solution)/shard_map/ppermute | solution.py:205
  3.2 6.4 %copy-start = (bf16[3,512,512]{2,1,0:T(8,128)(2,1)S(1)}, bf16[3,512,512]{2,1,0:T(8,128)(2,1)}, u32[]{:S(2)}) copy-start(bf16[3,512,512]{2,1,0:T(8,128)(2,1)} %left.5) | copy-start | bytes 4718596
  3.2 6.4 %copy-start.1 = (bf16[3,512,512]{2,1,0:T(8,128)(2,1)S(1)}, bf16[3,512,512]{2,1,0:T(8,128)(2,1)}, u32[]{:S(2)}) copy-start(bf16[3,512,512]{2,1,0:T(8,128)(2,1)} %right.5) | copy-start | bytes 4718596
  3.2 6.4 %copy-start.2 = (bf16[1,512,512]{2,1,0:T(8,128)(2,1)S(1)}, bf16[1,512,512]{2,1,0:T(8,128)(2,1)}, u32[]{:S(2)}) copy-start(bf16[1,512,512]{2,1,0:T(8,128)(2,1)} %own_block.1) | copy-start | bytes 1572868
  3.2 6.4 %copy-start.3 = (s32[16]{0:T(128)S(1)}, s32[16]{0:T(128)}, u32[]{:S(2)}) copy-start(s32[16]{0:T(128)} %sizes.1) | copy-start | bytes 196
  4.1 12.2 %collective-permute-start.2 = (s32[4,3]{1,0:T(4,128)S(1)}, s32[4,3]{1,0:T(4,128)S(1)}, u32[]{:S(2)}, u32[]{:S(2)}) collective-permute-start(s32[4,3]{1,0:T(4,128)S(1)} %codes.1.own_codes), channel_id=1, source_target_pairs={{1,2},{2,1},{3,4},{4,3},{5,6},{6,5},{7,8},{8,7},{9,10},{10,9},{11,... | collective-permute-start | bytes 152 | tf_op jit(solution)/shard_map/ppermute | solution.py:217
  7.3 2.3 %collective-permute-start = (s32[4,3]{1,0:T(4,128)S(1)}, s32[4,3]{1,0:T(4,128)S(1)}, u32[]{:S(2)}, u32[]{:S(2)}) collective-permute-start(s32[4,3]{1,0:T(4,128)S(1)} %codes.1.own_codes), channel_id=1, source_target_pairs={{0,1},{1,0},{2,3},{3,2},{4,5},{5,4},{6,7},{7,6},{8,9},{9,8},{10,11... | collective-permute-start | bytes 152 | tf_op jit(solution)/shard_map/ppermute | solution.py:216
  17.1 8.5 %collective-permute-start.4 = (bf16[256,512]{1,0:T(8,128)(2,1)S(1)}, bf16[256,512]{1,0:T(8,128)(2,1)S(1)}, u32[]{:S(2)}, u32[]{:S(2)}) collective-permute-start(bf16[256,512]{1,0:T(8,128)(2,1)S(1)} %far_theirs.1), channel_id=1, source_target_pairs={{0,16},{16,0},{1,17},{17,1},{2,18},{18,2},{3,19},{19,3},{4,20},{20... | collective-permute-start | bytes 786440 | tf_op jit(solution)/shard_map/ppermute | solution.py:247

commit v8 on v7

--- a/solution.py
+++ b/solution.py
@@ -154,7 +154,10 @@
 
             @pl.when(rest_forward & rest_adjoint)
             def _():
-                acc[...] += forward_one() + adjoint_one()
+                a = jnp.concatenate([forward_left(forwards - 1), adjoint_left(adjoints - 1).T], axis=0)
+                middle = dot(a, clean[...], 1, 0).astype(BF16)
+                acc[...] += (dot(middle[:share], right[rights[forwards - 1]], 1, 0)
+                             + dot(middle[share:], adjoint_right(adjoints - 1), 1, 1))
 
             @pl.when(rest_forward & ~rest_adjoint)
             def _():

time: 26.5 us -> 26.5 us (level)
  no operation moved by 1% of the time
where the time goes in v8:
time: 26.5 us; the launch traced here: 26.4 us
  waiting for transfers between devices  11.1 us (42%)
  starting transfers between devices  8.5 us (32%)
  Pallas kernels  6.04 us (23%)
  between operations  0.73 us (3%)
    ppermute x1, waiting for transfers between devices, shards(): got = [lax.ppermute(theirs, 'group', hops[0])]  6.33 us
    ppermute x1, waiting for transfers between devices, shards(): other_codes = lax.ppermute(codes, 'sector', others)  3.9 us
    ppermute x1, starting transfers between devices, shards(): other_codes = lax.ppermute(codes, 'sector', others)  3.13 us
    pallas_call x1, Pallas kernels, shards(): pl.pallas_call(near_kernel, out_shape=[jax.ShapeDtypeStruct((width, width...  2.85 us
    ppermute x1, starting transfers between devices, shards(): other_block = lax.ppermute(wavefunction, 'sector', others)  2.54 us
    pallas_call x2, Pallas kernels, far(): pl.pallas_call(functools.partial(far_kernel, mine), out_shape=jax.ShapeDt...  1.54 us
    ppermute x1, starting transfers between devices, shards(): friend_codes = lax.ppermute(codes, 'sector', friends)  1.47 us
    ppermute x1, starting transfers between devices, shards(): got = [lax.ppermute(theirs, 'group', hops[0])]  1.36 us
  transfers between devices with their start and end apart: 5, of which 3 were waited for; matrix products, arithmetic and copies ran while one was open for 0% of the time, Pallas kernels for 17%

profile of v8, /device:TPU:22, one launch (start us, length us, event | category | flops | bytes accessed | tf_op | source)
XLA Modules:
  0.0 26.4 jit_solution(6927709583999128143)
XLA Ops:
  0.0 0.0 collective-permute-start.1
  0.0 2.5 %collective-permute-start.3 = (bf16[1,512,512]{2,1,0:T(8,128)(2,1)}, bf16[1,512,512]{2,1,0:T(8,128)(2,1)S(1)}, u32[]{:S(2)}, u32[]{:S(2)}) collective-permute-start(bf16[1,512,512]{2,1,0:T(8,128)(2,1)} %own_block.1), channel_id=1, source_target_pairs={{1,2},{2,1},{3,4},{4,3},{5,6},{6,5},{7,8},{8,7},{9,10},{10,9},{11,... | collective-permute-start | bytes 1572872 | tf_op jit(solution)/shard_map/ppermute | solution.py:208
  3.2 0.0 copy-start
  3.2 0.0 copy-start.1
  3.2 0.0 copy-start.2
  3.2 0.0 copy-start.3
  3.2 0.9 %codes.1.own_codes = s32[4,3]{1,0:T(4,128)S(1)} custom-call(s32[4,3]{1,0:T(4,128)} %term_list.1, s32[1,1]{1,0:T(1,128)} %bitcast.1.term_counts), custom_call_target="tpu_custom_call" | custom-call | flops 4000000000 | bytes 16777216 | tf_op jit(solution)/shard_map/codes/pallas_call | solution.py:210
  4.1 3.1 %collective-permute-start.2 = (s32[4,3]{1,0:T(4,128)S(1)}, s32[4,3]{1,0:T(4,128)S(1)}, u32[]{:S(2)}, u32[]{:S(2)}) collective-permute-start(s32[4,3]{1,0:T(4,128)S(1)} %codes.1.own_codes), channel_id=1, source_target_pairs={{1,2},{2,1},{3,4},{4,3},{5,6},{6,5},{7,8},{8,7},{9,10},{10,9},{11,... | collective-permute-start | bytes 152 | tf_op jit(solution)/shard_map/ppermute | solution.py:220
  7.3 1.5 %collective-permute-start = (s32[4,3]{1,0:T(4,128)S(1)}, s32[4,3]{1,0:T(4,128)S(1)}, u32[]{:S(2)}, u32[]{:S(2)}) collective-permute-start(s32[4,3]{1,0:T(4,128)S(1)} %codes.1.own_codes), channel_id=1, source_target_pairs={{0,1},{1,0},{2,3},{3,2},{4,5},{5,4},{6,7},{7,6},{8,9},{9,8},{10,11... | collective-permute-start | bytes 152 | tf_op jit(solution)/shard_map/ppermute | solution.py:219
  8.8 0.8 %collective-permute-done.friend_codes = s32[4,3]{1,0:T(4,128)S(1)} collective-permute-done((s32[4,3]{1,0:T(4,128)S(1)}, s32[4,3]{1,0:T(4,128)S(1)}, u32[]{:S(2)}, u32[]{:S(2)}) %collective-permute-start) | collective-permute-done | bytes 80 | tf_op jit(solution)/shard_map/ppermute | solution.py:219
  9.6 0.0 collective-permute-done.1.friend_block
  9.6 0.0 copy-done
  9.6 0.0 copy-done.1
  9.6 0.0 copy-done.2
  9.6 0.0 copy-done.3
  9.6 2.9 %near.1 = (f32[512,512]{1,0:T(8,128)S(1)}, s32[1,11]{1,0:T(1,128)S(1)}) custom-call(s32[4,3]{1,0:T(4,128)S(1)} %codes.1.own_codes, s32[4,3]{1,0:T(4,128)S(1)} %collective-permute-done.friend_codes, s32[16]{0:T(128)S(1)} %copy-done.3, bf16[1,512,512]{2,1,0:T(8,128)(2,1)S(1)} %copy-done.2, bf16[1,512,512]{2,1,0:T(8,128)(2,1)S(1)} %collective-permute-done.1.friend_block, ...), custom_call_target="tpu_custom_call" | custom-call | tf_op jit(solution)/shard_map/near/pallas_call | solution.py:223
  12.5 3.9 %collective-permute-done.2.other_codes = s32[4,3]{1,0:T(4,128)S(1)} collective-permute-done((s32[4,3]{1,0:T(4,128)S(1)}, s32[4,3]{1,0:T(4,128)S(1)}, u32[]{:S(2)}, u32[]{:S(2)}) %collective-permute-start.2) | collective-permute-done | bytes 80 | tf_op jit(solution)/shard_map/ppermute | solution.py:220
  16.4 0.0 collective-permute-done.3.other_block
  16.4 0.8 %far_theirs.1 = bf16[256,512]{1,0:T(8,128)(2,1)S(1)} custom-call(s32[1,11]{1,0:T(1,128)S(1)} %get-tuple-element.7.plan, s32[4,3]{1,0:T(4,128)S(1)} %collective-permute-done.2.other_codes, bf16[1,512,512]{2,1,0:T(8,128)(2,1)S(1)} %collective-permute-done.3.other_block, bf16[3,512,512]{2,1,0:T(8,128)(2,1)S(1)} %copy-done, bf16[3,512,512]{2,1,0:T(8,128)(2,1)S(1)} %copy-done.1, ...), custom_call_target="tpu_custom_call" | custom-call | tf_op jit(solution)/shard_map/far_theirs/pallas_call | solution.py:237
  17.1 1.4 %collective-permute-start.4 = (bf16[256,512]{1,0:T(8,128)(2,1)S(1)}, bf16[256,512]{1,0:T(8,128)(2,1)S(1)}, u32[]{:S(2)}, u32[]{:S(2)}) collective-permute-start(bf16[256,512]{1,0:T(8,128)(2,1)S(1)} %far_theirs.1), channel_id=1, source_target_pairs={{0,16},{16,0},{1,17},{17,1},{2,18},{18,2},{3,19},{19,3},{4,20},{20... | collective-permute-start | bytes 786440 | tf_op jit(solution)/shard_map/ppermute | solution.py:250
  18.5 0.8 %far_mine.1.kept = f32[256,512]{1,0:T(8,128)S(1)} custom-call(s32[1,11]{1,0:T(1,128)S(1)} %get-tuple-element.7.plan, s32[4,3]{1,0:T(4,128)S(1)} %collective-permute-done.2.other_codes, bf16[1,512,512]{2,1,0:T(8,128)(2,1)S(1)} %collective-permute-done.3.other_block, bf16[3,512,512]{2,1,0:T(8,128)(2,1)S(1)} %copy-done, bf16[3,512,512]{2,1,0:T(8,128)(2,1)S(1)} %copy-done.1, ...), custom_call_target="tpu_custom_call" | custom-call | tf_op jit(solution)/shard_map/far_mine/pallas_call | solution.py:237
  19.3 6.3 %collective-permute-done.4.refs_0_ = bf16[256,512]{1,0:T(8,128)(2,1)S(1)} collective-permute-done((bf16[256,512]{1,0:T(8,128)(2,1)S(1)}, bf16[256,512]{1,0:T(8,128)(2,1)S(1)}, u32[]{:S(2)}, u32[]{:S(2)}) %collective-permute-start.4) | collective-permute-done | bytes 262176 | tf_op jit(solution)/shard_map/ppermute | solution.py:250
  25.6 0.7 %last.1 = bf16[1,256,512]{2,1,0:T(8,128)(2,1)} custom-call(f32[256,512]{1,0:T(8,128)S(1)} %far_mine.1.kept, bf16[256,512]{1,0:T(8,128)(2,1)S(1)} %collective-permute-done.4.refs_0_), custom_call_target="tpu_custom_call" | custom-call | tf_op jit(solution)/shard_map/last/pallas_call | solution.py:260
Async XLA Ops:
  0.0 9.6 %collective-permute-start.1 = (bf16[1,512,512]{2,1,0:T(8,128)(2,1)}, bf16[1,512,512]{2,1,0:T(8,128)(2,1)S(1)}, u32[]{:S(2)}, u32[]{:S(2)}) collective-permute-start(bf16[1,512,512]{2,1,0:T(8,128)(2,1)} %own_block.1), channel_id=1, source_target_pairs={{0,1},{1,0},{2,3},{3,2},{4,5},{5,4},{6,7},{7,6},{8,9},{9,8},{10,11... | collective-permute-start | bytes 1572872 | tf_op jit(solution)/shard_map/ppermute | solution.py:209
  0.0 16.4 %collective-permute-start.3 = (bf16[1,512,512]{2,1,0:T(8,128)(2,1)}, bf16[1,512,512]{2,1,0:T(8,128)(2,1)S(1)}, u32[]{:S(2)}, u32[]{:S(2)}) collective-permute-start(bf16[1,512,512]{2,1,0:T(8,128)(2,1)} %own_block.1), channel_id=1, source_target_pairs={{1,2},{2,1},{3,4},{4,3},{5,6},{6,5},{7,8},{8,7},{9,10},{10,9},{11,... | collective-permute-start | bytes 1572872 | tf_op jit(solution)/shard_map/ppermute | solution.py:208
  3.2 6.4 %copy-start = (bf16[3,512,512]{2,1,0:T(8,128)(2,1)S(1)}, bf16[3,512,512]{2,1,0:T(8,128)(2,1)}, u32[]{:S(2)}) copy-start(bf16[3,512,512]{2,1,0:T(8,128)(2,1)} %left.5) | copy-start | bytes 4718596
  3.2 6.4 %copy-start.1 = (bf16[3,512,512]{2,1,0:T(8,128)(2,1)S(1)}, bf16[3,512,512]{2,1,0:T(8,128)(2,1)}, u32[]{:S(2)}) copy-start(bf16[3,512,512]{2,1,0:T(8,128)(2,1)} %right.5) | copy-start | bytes 4718596
  3.2 6.4 %copy-start.2 = (bf16[1,512,512]{2,1,0:T(8,128)(2,1)S(1)}, bf16[1,512,512]{2,1,0:T(8,128)(2,1)}, u32[]{:S(2)}) copy-start(bf16[1,512,512]{2,1,0:T(8,128)(2,1)} %own_block.1) | copy-start | bytes 1572868
  3.2 6.4 %copy-start.3 = (s32[16]{0:T(128)S(1)}, s32[16]{0:T(128)}, u32[]{:S(2)}) copy-start(s32[16]{0:T(128)} %sizes.1) | copy-start | bytes 196
  4.1 12.2 %collective-permute-start.2 = (s32[4,3]{1,0:T(4,128)S(1)}, s32[4,3]{1,0:T(4,128)S(1)}, u32[]{:S(2)}, u32[]{:S(2)}) collective-permute-start(s32[4,3]{1,0:T(4,128)S(1)} %codes.1.own_codes), channel_id=1, source_target_pairs={{1,2},{2,1},{3,4},{4,3},{5,6},{6,5},{7,8},{8,7},{9,10},{10,9},{11,... | collective-permute-start | bytes 152 | tf_op jit(solution)/shard_map/ppermute | solution.py:220
  7.3 2.3 %collective-permute-start = (s32[4,3]{1,0:T(4,128)S(1)}, s32[4,3]{1,0:T(4,128)S(1)}, u32[]{:S(2)}, u32[]{:S(2)}) collective-permute-start(s32[4,3]{1,0:T(4,128)S(1)} %codes.1.own_codes), channel_id=1, source_target_pairs={{0,1},{1,0},{2,3},{3,2},{4,5},{5,4},{6,7},{7,6},{8,9},{9,8},{10,11... | collective-permute-start | bytes 152 | tf_op jit(solution)/shard_map/ppermute | solution.py:219
  17.1 8.5 %collective-permute-start.4 = (bf16[256,512]{1,0:T(8,128)(2,1)S(1)}, bf16[256,512]{1,0:T(8,128)(2,1)S(1)}, u32[]{:S(2)}, u32[]{:S(2)}) collective-permute-start(bf16[256,512]{1,0:T(8,128)(2,1)S(1)} %far_theirs.1), channel_id=1, source_target_pairs={{0,16},{16,0},{1,17},{17,1},{2,18},{18,2},{3,19},{19,3},{4,20},{20... | collective-permute-start | bytes 786440 | tf_op jit(solution)/shard_map/ppermute | solution.py:250
